TPU v7x, 512 devices: a whole 4x8x8 slice. The times are simulated.
512 devices in a mesh: row: 32 (over y_hi, z), proto: 16 (over x, y_lo, core).
Axes of the slice: x: 4, y: 8 (y_hi: 4, y_lo: 2; y = y_hi * 2 + y_lo), z: 8, core: 2. Of those that a mesh axis runs over, the one named last changes fastest.
Arguments:
- embeddings: bfloat16 [8192, 128], P('row'), may hold values from -6.75 to 6.75
- second_view: bfloat16 [8192, 128], P('row'), may hold values from -6.75 to 6.75
- prototypes: bfloat16 [65536, 128], P('proto'), may hold values from -6.75 to 6.75
- row_scale: float32 [8192], P('row'), may hold values from 1 to 16, as said below
- col_scale: float32 [65536], P('proto'), may hold values from 1 to 16, as said below
Outputs:
- embed_grad: float32 [8192, 128], P(('row', 'proto'))
- proto_grad: float32 [65536, 128], P(('proto', 'row'))
Inputs may be any that keep to these rules, and one draw needn't show every extreme that they name: `row_scale`: positive scalings. `col_scale`: positive scalings.
All inputs are finite; a program needn't handle non-finite values.
Results may differ from a plain program's by a relative error of at most 0.0025.
Values may be sent and summed in bfloat16 or wider, within the bound.
A program may use at most 64 MiB of HBM per device.

v0:
```python
import jax
import jax.numpy as jnp
from jax import lax
from jax.sharding import PartitionSpec as P

ITERS = 4


def contract_rows(left, right):
    return lax.dot_general(
        left, right, (((0,), (0,)), ((), ())), preferred_element_type=jnp.float32
    )


def contract_width(left, right):
    return lax.dot_general(
        left, right, (((1,), (1,)), ((), ())), preferred_element_type=jnp.float32
    )


def per_device(embeddings, second_view, prototypes, row_scale, col_scale):
    feat_width = embeddings.shape[1]
    proto_count = prototypes.shape[0]
    logit_scale = 1.0 / (0.05 * feat_width)
    view_scale = 1.0 / (0.1 * feat_width)
    plan_mass = 64.0 * proto_count * lax.axis_size("proto")

    def make_plan():
        logits = contract_width(embeddings, prototypes) * logit_scale
        return row_scale[:, None] * col_scale[None, :] * jnp.exp(logits) / plan_mass

    def make_cot():
        return -contract_width(second_view, prototypes) * view_scale

    stored_plan = make_plan()
    cotangent = make_cot()
    weighted = stored_plan * cotangent

    def plan_now():
        return make_plan()

    row_mass, row_weight = lax.psum((stored_plan.sum(1), weighted.sum(1)), "proto")
    row_dual = row_weight / row_mass
    col_mass, col_weight = lax.psum((stored_plan.sum(0), weighted.sum(0)), "row")

    def solve_cols(duals_rows):
        product = lax.psum(jnp.dot(duals_rows, plan_now(), precision=lax.Precision.HIGHEST), "row")
        return (col_weight - product) / col_mass

    col_dual = solve_cols(row_dual)
    for sweep in range(ITERS - 1):
        product = lax.psum(jnp.dot(plan_now(), col_dual, precision=lax.Precision.HIGHEST), "proto")
        row_dual = (row_weight - product) / row_mass
        col_dual = solve_cols(row_dual)
    final_plan, final_cot = (make_plan(), make_cot())
    logit_grad = final_plan * (final_cot - row_dual[:, None] - col_dual[None, :])
    scaled_grad = (logit_scale * logit_grad).astype(jnp.bfloat16)
    scaled_plan = (-view_scale * final_plan).astype(jnp.bfloat16)
    embed_grad = lax.psum_scatter(
        jnp.dot(scaled_grad, prototypes, preferred_element_type=jnp.float32),
        "proto",
        scatter_dimension=0,
        tiled=True,
    )
    stacked = jnp.concatenate((scaled_grad, scaled_plan), 0)
    sources = jnp.concatenate((embeddings, second_view), 0)
    proto_grad = lax.psum_scatter(
        contract_rows(stacked, sources), "row", scatter_dimension=0, tiled=True
    )
    return (embed_grad, proto_grad)


def solution(mesh):
    return jax.shard_map(
        per_device,
        mesh=mesh,
        in_specs=(P("row", None), P("row", None), P("proto", None), P("row"), P("proto")),
        out_specs=(P(("row", "proto"), None), P(("proto", "row"), None)),
        check_vma=False,
    )
```

profile of v0, /device:TPU:1, one launch (start us, length us, event | category | flops | bytes accessed | tf_op | source)
XLA Modules:
  0.0 1080.3 jit_solution(11245116675598459363)
XLA Ops:
  7.2 0.0 copy-start
  7.2 0.0 copy-start.2
  7.2 0.0 reduce-scatter.3.cloned.1.call-start
  7.2 1.2 copy-done
  8.4 1.7 fusion.2
  10.1 0.0 copy-done.2
  10.1 0.0 copy-start.1
  10.1 3.3 multiply_reduce_fusion.1
  13.5 0.0 copy-done.1
  13.5 33.3 %all-reduce.1 = (f32[256]{0:T(256)S(1)}, f32[256]{0:T(256)S(1)}) all-reduce(f32[256]{0:T(256)S(1)} %get-tuple-element.2, f32[256]{0:T(256)S(1)} %get-tuple-element.4), channel_id=1, replica_groups=mesh['row'=32,'proto'=16] {'proto'}, use_global_device_ids=true, to_apply=%region_1.0 | all-reduce | flops 512 | bytes 4096 | tf_op jit(solution)/shard_map/psum | solution.py:42
  46.8 4.3 fusion.14
  51.1 131.6 %all-reduce = (f32[4096]{0:T(1024)S(1)}, f32[4096]{0:T(1024)S(1)}, f32[4096]{0:T(1024)S(1)}) all-reduce(f32[4096]{0:T(1024)S(1)} %get-tuple-element.5, f32[4096]{0:T(1024)S(1)} %get-tuple-element.3, f32[4096]{0:T(1024)S(1)} %bitcast.27), channel_id=1, replica_groups=mesh['row'=32,'proto'=16] {'row'}, use_global_device_ids=true, to_apply=%region_8.0 | all-reduce | flops 12288 | bytes 98304 | tf_op jit(solution)/shard_map/psum | solution.py:44
  182.8 5.5 fusion.12
  188.3 57.3 %psum.82 = f32[256]{0:T(256)S(1)} all-reduce(f32[256]{0:T(256)S(1)} %bitcast.36), channel_id=1, replica_groups=mesh['row'=32,'proto'=16] {'proto'}, use_global_device_ids=true, to_apply=%region_9.0 | all-reduce | flops 256 | bytes 2048 | tf_op jit(solution)/shard_map/psum | solution.py:52
  245.6 4.3 fusion.11
  249.9 124.4 %psum.83 = f32[4096]{0:T(1024)S(1)} all-reduce(f32[4096]{0:T(1024)S(1)} %bitcast.28), channel_id=1, replica_groups=mesh['row'=32,'proto'=16] {'row'}, use_global_device_ids=true, to_apply=%region_10.0 | all-reduce | flops 4096 | bytes 32768 | tf_op jit(solution)/shard_map/psum | solution.py:47
  374.3 5.5 fusion.10
  379.9 55.0 %psum.84 = f32[256]{0:T(256)S(1)} all-reduce(f32[256]{0:T(256)S(1)} %bitcast.37), channel_id=1, replica_groups=mesh['row'=32,'proto'=16] {'proto'}, use_global_device_ids=true, to_apply=%region_11.0 | all-reduce | flops 256 | bytes 2048 | tf_op jit(solution)/shard_map/psum | solution.py:52
  434.9 4.3 fusion.9
  439.2 124.2 %psum.85 = f32[4096]{0:T(1024)S(1)} all-reduce(f32[4096]{0:T(1024)S(1)} %bitcast.29), channel_id=1, replica_groups=mesh['row'=32,'proto'=16] {'row'}, use_global_device_ids=true, to_apply=%region_12.0 | all-reduce | flops 4096 | bytes 32768 | tf_op jit(solution)/shard_map/psum | solution.py:47
  563.5 5.5 fusion.8
  569.0 55.0 %psum.86 = f32[256]{0:T(256)S(1)} all-reduce(f32[256]{0:T(256)S(1)} %bitcast.38), channel_id=1, replica_groups=mesh['row'=32,'proto'=16] {'proto'}, use_global_device_ids=true, to_apply=%region_13.0 | all-reduce | flops 256 | bytes 2048 | tf_op jit(solution)/shard_map/psum | solution.py:52
  624.0 4.3 fusion.7
  628.4 124.4 %psum.87 = f32[4096]{0:T(1024)S(1)} all-reduce(f32[4096]{0:T(1024)S(1)} %bitcast.30), channel_id=1, replica_groups=mesh['row'=32,'proto'=16] {'row'}, use_global_device_ids=true, to_apply=%region_14.0 | all-reduce | flops 4096 | bytes 32768 | tf_op jit(solution)/shard_map/psum | solution.py:47
  752.8 0.0 copy-start.3
  752.8 6.1 multiply_convert_fusion
  759.0 1.4 fusion.27
  760.3 0.0 reduce-scatter.3.cloned.1.call-update
  760.3 0.0 reduce-scatter.5.cloned.1.call-start
  760.4 0.0 copy-done.3
  760.4 4.2 fusion.3
  764.6 0.0 reduce-scatter.5.cloned.1.call-update
  764.7 78.5 %reduce-scatter.3.cloned.1.call-done = f32[16,128]{1,0:T(8,128)} async-done(((f32[256,128]{1,0:T(8,128)}), f32[16,128]{1,0:T(8,128)}) %reduce-scatter.3.cloned.1.call-update) | async-done | bytes 8208 | tf_op jit(solution)/shard_map/reduce_scatter | solution.py:59
  843.1 230.3 %reduce-scatter.5.cloned.1.call-done = f32[128,128]{1,0:T(8,128)} async-done(((f32[4096,128]{1,0:T(8,128)}), f32[128,128]{1,0:T(8,128)}) %reduce-scatter.5.cloned.1.call-update) | async-done | bytes 65552 | tf_op jit(solution)/shard_map/reduce_scatter | solution.py:67
  (8 shorter events, 0.1 us)
Async XLA Ops:
  7.2 1.2 copy-start
  7.2 2.9 copy-start.2
  7.2 836.0 %reduce-scatter.3.cloned.1.call-start = ((), (), s32[]{:S(2)}) async-start(), calls=%async_computation.2 | async-start | bytes 139264 | tf_op jit(solution)/shard_map/reduce_scatter | solution.py:59
  10.1 3.3 copy-start.1
  752.8 7.6 copy-start.3
  760.3 313.1 %reduce-scatter.5.cloned.1.call-start = ((), (), s32[]{:S(2)}) async-start(), calls=%async_computation.3 | async-start | bytes 2162688 | tf_op jit(solution)/shard_map/reduce_scatter | solution.py:67
Sparse Core Ops, SparseCore 0:
  760.5 82.6 reduce-scatter.2
  848.1 225.2 reduce-scatter.4
where the time goes:
time: 1080 us
  blocking collectives  705 us (65%)
  waiting for transfers between devices  309 us (29%)
  matrix products  44.6 us (4%)
  between operations  14.1 us (1%)
    psum x3, blocking collectives, solve_cols(): lax.psum(jnp.dot(duals_rows, plan_now(), precision=lax.Precision.HIGHEST)...  373 us
    reduce_scatter x1, waiting for transfers between devices, per_device(): lax.psum_scatter(contract_rows(stacked, sources), 'row', scatter_dimensio...  230 us
    psum x3, blocking collectives, per_device(): lax.psum(jnp.dot(plan_now(), col_dual, precision=lax.Precision.HIGHEST),...  167 us
    psum x1, blocking collectives, per_device(): lax.psum((stored_plan.sum(0), weighted.sum(0)), 'row')  132 us
    reduce_scatter x1, waiting for transfers between devices, per_device(): lax.psum_scatter(jnp.dot(scaled_grad, prototypes, preferred_element_type=...  78.5 us
    psum x1, blocking collectives, per_device(): lax.psum((stored_plan.sum(1), weighted.sum(1)), 'proto')  33.3 us
  transfers between devices with their start and end apart: 2, of which 2 were waited for; matrix products, arithmetic and copies ran while one was open for 0% of the time, Pallas kernels for 0%

commit v1 on v0

v1 whole, which is shorter than its diff:
```python
import functools

import jax
import jax.numpy as jnp
from jax import lax
from jax.experimental import pallas as pl
from jax.experimental.pallas import tpu as pltpu
from jax.sharding import PartitionSpec as P

ITERS = 4
LANES = 128
MESH = pl.DeviceIdType.MESH
F32 = jnp.float32
BF16 = jnp.bfloat16

DIMS = (4, 2, 2, 4, 8)


def dot_nt(left, right):
    return lax.dot_general(left, right, (((1,), (1,)), ((), ())), preferred_element_type=F32)


def dot_tn(left, right):
    return lax.dot_general(left, right, (((0,), (0,)), ((), ())), preferred_element_type=F32)


def down(row, height=LANES):
    return jnp.broadcast_to(row, (height, LANES)).T


def fold(block):
    return block.reshape(block.shape[0] // 8, 8, LANES).sum(0)


def kernel(
    dims,
    proto_total,
    emb_in,
    view_in,
    pro_in,
    rs_in,
    cs_in,
    eg_ref,
    pg_ref,
    ev,
    pr,
    rs,
    cs,
    plan,
    cot,
    lg,
    grad,
    splan,
    tail,
    colm,
    colw,
    bx0,
    by0,
    bz0,
    bx,
    by,
    bz,
    eb,
    fy,
    fx_out,
    fx,
    pb,
    fz,
    local_sem,
    g_send,
    g_recv,
    r_send,
    r_recv,
    c_send,
    c_recv,
    x_send,
    y_send,
    z_send,
    z0_send,
    x_recv,
    y_recv,
    z_recv,
    fx_send,
    fy_send,
    fz_send,
    fx_recv,
    fy_recv,
    fz_recv,
):
    nx, nyl, nc, nyh, nz = dims
    ny, nxc = nyl * nyh, nx * nc
    row_id, proto_id = lax.axis_index("row"), lax.axis_index("proto")
    yh, z = row_id // nz, row_id % nz
    core = proto_id % nc
    yl = (proto_id // nc) % nyl
    x = proto_id // (nc * nyl)
    y = yh * nyl + yl
    xc = x * nc + core

    def at_z(other):
        return (yh * nz + other, proto_id)

    def at_y(other):
        return ((other // nyl) * nz + z, (x * nyl + other % nyl) * nc + core)

    def at_xc(other):
        return (row_id, ((other // nc) * nyl + yl) * nc + other % nc)

    chunks, groups = plan.shape[0] // LANES, plan.shape[1] // LANES
    per_block = chunks // nyh
    width = emb_in.shape[-1]
    logit_scale = 1.0 / (0.05 * width)
    view_scale = 1.0 / (0.1 * width)
    mass_inverse = 1.0 / (64.0 * proto_total)

    own = pl.ds(yh * per_block, per_block)
    loads = [
        pltpu.make_async_copy(emb_in, ev.at[0, own], local_sem.at[0]),
        pltpu.make_async_copy(view_in, ev.at[1, own], local_sem.at[1]),
        pltpu.make_async_copy(rs_in, rs.at[own], local_sem.at[2]),
        pltpu.make_async_copy(cs_in.at[yh], cs, local_sem.at[3]),
        pltpu.make_async_copy(pro_in.at[yh], pr, local_sem.at[4]),
    ]
    for load in loads:
        load.start()

    barrier = pltpu.get_barrier_semaphore()
    for step in range(1, nz):
        pl.semaphore_signal(barrier, inc=1, device_id=at_z((z + step) % nz), device_id_type=MESH)
    for step in range(1, ny):
        pl.semaphore_signal(barrier, inc=1, device_id=at_y((y + step) % ny), device_id_type=MESH)
    for step in range(1, nxc):
        pl.semaphore_signal(barrier, inc=1, device_id=at_xc((xc + step) % nxc), device_id_type=MESH)
    for load in loads:
        load.wait()
    pl.semaphore_wait(barrier, nz + ny + nxc - 3)

    sign = 2 * yl - 1
    blocks = []
    sends = []
    for step in range(1, nyh):
        target = (y + sign * step + ny) % ny
        source = (y + (sign if step % 2 else -sign) * step + ny) % ny
        there = pl.ds((source // nyl) * per_block, per_block)
        blocks.append((source // nyl, there))
        rows_out = pltpu.make_async_remote_copy(
            ev.at[core, own], ev.at[core, own], g_send.at[step], g_recv.at[step], at_y(target), MESH
        )
        scale_out = pltpu.make_async_remote_copy(
            rs.at[own], rs.at[own], r_send.at[step], r_recv.at[step], at_y(target), MESH
        )
        rows_out.start()
        scale_out.start()
        sends += [rows_out, scale_out]

    colm[...] = jnp.zeros_like(colm)
    colw[...] = jnp.zeros_like(colw)

    def first_chunk(i):
        rows = pl.ds(pl.multiple_of(i * LANES, LANES), LANES)
        lg[...] = dot_nt(ev[0, i], pr[...])
        cot[rows, :] = dot_nt(ev[1, i], pr[...]) * -view_scale
        scale = down(rs[i]) * mass_inverse
        mass = jnp.zeros((LANES, LANES), F32)
        weight = jnp.zeros((LANES, LANES), F32)
        for k in range(groups):
            cols = slice(k * LANES, (k + 1) * LANES)
            value = scale * cs[k : k + 1, :] * jnp.exp(lg[:, cols] * logit_scale)
            plan[rows, cols] = value
            weighted = value * cot[rows, cols]
            mass = mass + value
            weight = weight + weighted
            colm[k] += fold(value)
            colw[k] += fold(weighted)
        bx0[xc, 0, pl.ds(i, 1), :] = mass.T.sum(0, keepdims=True)
        bx0[xc, 1, pl.ds(i, 1), :] = weight.T.sum(0, keepdims=True)

    def first_block(block):
        @pl.loop(0, per_block)
        def _(part):
            first_chunk(block * per_block + part)

    first_block(yh)
    partner = at_xc(x * nc + (core + 1) % nc)
    for step, (block, there) in enumerate(blocks, 1):
        pltpu.make_async_remote_copy(
            ev.at[core, there], ev.at[core, there], g_send.at[step], g_recv.at[step], partner, MESH
        ).wait_recv()
        hand = pltpu.make_async_remote_copy(
            ev.at[core, there], ev.at[core, there], c_send.at[step], c_recv.at[step], partner, MESH
        )
        hand.start()
        sends.append(hand)
        pltpu.make_async_remote_copy(
            rs.at[there], rs.at[there], r_send.at[step], r_recv.at[step], partner, MESH
        ).wait_recv()
        taken = ev.at[(core + 1) % nc, there]
        pltpu.make_async_remote_copy(
            taken, taken, c_send.at[step], c_recv.at[step], partner, MESH
        ).wait_recv()
        first_block(block)

    def start(slots, me, count, address, send, recv):
        for step in range(1, count):
            other = (me + step) % count
            pltpu.make_async_remote_copy(
                slots.at[me], slots.at[me], send.at[step], recv.at[me], address(other), MESH
            ).start()

    def finish(slots, me, count, address, send, recv):
        for step in range(1, count):
            other = (me + step) % count
            pltpu.make_async_remote_copy(
                slots.at[other], slots.at[other], send.at[step], recv.at[other], address(other), MESH
            ).wait_recv()
        for step in range(1, count):
            other = (me + step) % count
            pltpu.make_async_remote_copy(
                slots.at[me], slots.at[me], send.at[step], recv.at[me], address(other), MESH
            ).wait_send()

    def total(slots, count):
        result = slots[0]
        for slot in range(1, count):
            result = result + slots[slot]
        return result

    along_x = (xc, nxc, at_xc)
    along_y = (y, ny, at_y)
    along_z = (z, nz, at_z)

    start(bx0, *along_x, x_send, x_recv.at[0])
    for k in range(groups):
        bz0[z, 0, k : k + 1, :] = colm[k].sum(0, keepdims=True)
        bz0[z, 1, k : k + 1, :] = colw[k].sum(0, keepdims=True)
    start(bz0, *along_z, z0_send, z_recv.at[0])

    @pl.loop(0, chunks)
    def _(i):
        rows = pl.ds(pl.multiple_of(i * LANES, LANES), LANES)
        splan[rows, :] = (plan[rows, :] * -view_scale).astype(BF16)

    finish(bx0, *along_x, x_send, x_recv.at[0])
    by0[y] = total(bx0, nxc)
    start(by0, *along_y, y_send, y_recv.at[0])

    @pl.loop(0, groups)
    def _(k):
        cols = pl.ds(pl.multiple_of(k * LANES, LANES), LANES)
        tail[cols, :] = dot_tn(splan[:, cols], ev[1].reshape(chunks * LANES, width))

    finish(by0, *along_y, y_send, y_recv.at[0])
    row_sums = total(by0, ny)
    row_mass, row_weight = row_sums[0], row_sums[1]

    def column_part(row_dual, k):
        bx[k, xc] = row_dual
        tiles = tuple(jnp.zeros((8, LANES), F32) for _ in range(groups))

        def add(i, tiles):
            rows = pl.ds(pl.multiple_of(i * LANES, LANES), LANES)
            dual = down(bx[k, xc, pl.ds(i, 1), :])
            return tuple(
                tile + fold(plan[rows, g * LANES : (g + 1) * LANES] * dual)
                for g, tile in enumerate(tiles)
            )

        tiles = lax.fori_loop(0, chunks, add, tiles)
        for g, tile in enumerate(tiles):
            bz[k, z, g : g + 1, :] = tile.sum(0, keepdims=True)

    def row_part(col_dual, k):
        def one(i, unused):
            rows = pl.ds(pl.multiple_of(i * LANES, LANES), LANES)
            block = plan[rows, :LANES] * col_dual[0:1, :]
            for g in range(1, groups):
                block = block + plan[rows, g * LANES : (g + 1) * LANES] * col_dual[g : g + 1, :]
            bx[k, xc, pl.ds(i, 1), :] = block.T.sum(0, keepdims=True)
            return unused

        lax.fori_loop(0, chunks, one, 0)

    row_dual = row_weight / row_mass
    column_part(row_dual, ITERS - 1)
    start(bz.at[ITERS - 1], *along_z, z_send, z_recv.at[ITERS])
    finish(bz0, *along_z, z0_send, z_recv.at[0])
    col_sums = total(bz0, nz)
    col_mass, col_weight = col_sums[0], col_sums[1]
    finish(bz.at[ITERS - 1], *along_z, z_send, z_recv.at[ITERS])
    col_dual = (col_weight - total(bz.at[ITERS - 1], nz)) / col_mass

    def sweep(k, duals):
        row_part(duals[1], k)
        start(bx.at[k], *along_x, x_send, x_recv.at[k + 1])
        finish(bx.at[k], *along_x, x_send, x_recv.at[k + 1])
        by[k, y] = total(bx.at[k], nxc)
        start(by.at[k], *along_y, y_send, y_recv.at[k + 1])
        finish(by.at[k], *along_y, y_send, y_recv.at[k + 1])
        row_dual = (row_weight - total(by.at[k], ny)) / row_mass
        column_part(row_dual, k)
        start(bz.at[k], *along_z, z_send, z_recv.at[k + 1])
        finish(bz.at[k], *along_z, z_send, z_recv.at[k + 1])
        return row_dual, (col_weight - total(bz.at[k], nz)) / col_mass

    row_dual, col_dual = lax.fori_loop(0, ITERS - 1, sweep, (row_dual, col_dual))

    bx[0, xc] = row_dual
    half = nx // per_block

    def last_chunk(i, part, block):
        rows = pl.ds(pl.multiple_of(i * LANES, LANES), LANES)
        dual = down(bx[0, xc, pl.ds(i, 1), :])
        for g in range(groups):
            cols = slice(g * LANES, (g + 1) * LANES)
            piece = plan[rows, cols] * (cot[rows, cols] - dual - col_dual[g : g + 1, :])
            grad[rows, cols] = (logit_scale * piece).astype(BF16)
        product = jnp.dot(grad[rows, :], pr[...], preferred_element_type=F32)
        eb[block, pl.ds(part * half, half)] = product.reshape(
            half, nyl, LANES // (half * nyl), LANES
        ).astype(BF16)

    def send_rows(other, step):
        return pltpu.make_async_remote_copy(
            eb.at[other // nyl, :, other % nyl],
            fy.at[y],
            fy_send.at[step],
            fy_recv.at[y],
            at_y(other),
            MESH,
        )

    row_sends = []
    for step in range(1, nyh + 1):
        block = (yh + step) % nyh

        @pl.loop(0, per_block)
        def _(part):
            last_chunk(block * per_block + part, part, block)

        for low in range(nyl):
            if step < nyh:
                other, slot = block * nyl + low, step * nyl + low
            elif low:
                other, slot = yh * nyl + (yl + low) % nyl, low
            else:
                continue
            row_sends.append(send_rows(other, slot))
            row_sends[-1].start()

    proto_sends = []
    for step in range(1, nz + 1):
        other = (z + step) % nz
        cols = pl.ds(pl.multiple_of(other * LANES, LANES), LANES)
        share = tail[cols, :] + dot_tn(grad[:, cols], ev[0].reshape(chunks * LANES, width))
        if step < nz:
            pb[step] = share.astype(BF16)
            proto_sends.append(
                pltpu.make_async_remote_copy(
                    pb.at[step], fz.at[z], fz_send.at[step], fz_recv.at[z], at_z(other), MESH
                )
            )
            proto_sends[-1].start()
        else:
            pg_ref[...] = share

    def arrived(slots, me, count, recv, send, address):
        for step in range(1, count):
            other = (me + step) % count
            pltpu.make_async_remote_copy(
                slots.at[other], slots.at[other], send.at[step], recv.at[other], address(other), MESH
            ).wait_recv()

    arrived(fy, y, ny, fy_recv, fy_send, at_y)
    rows_sum = eb[yh, :, yl].astype(F32)
    for step in range(1, ny):
        rows_sum = rows_sum + fy[(y + step) % ny].astype(F32)
    fx_out[...] = rows_sum.reshape(fx_out.shape)
    last_sends = []
    for step in range(1, nxc):
        other = (xc + step) % nxc
        last_sends.append(
            pltpu.make_async_remote_copy(
                fx_out.at[other], fx.at[xc], fx_send.at[step], fx_recv.at[xc], at_xc(other), MESH
            )
        )
        last_sends[-1].start()

    arrived(fz, z, nz, fz_recv, fz_send, at_z)
    share = pg_ref[...]
    for step in range(1, nz):
        share = share + fz[(z + step) % nz].astype(F32)
    pg_ref[...] = share

    arrived(fx, xc, nxc, fx_recv, fx_send, at_xc)
    rows_out = fx_out[xc]
    for step in range(1, nxc):
        rows_out = rows_out + fx[(xc + step) % nxc]
    eg_ref[...] = rows_out

    for send in sends + row_sends + proto_sends + last_sends:
        send.wait_send()


def build(mesh, dims):
    nx, nyl, nc, nyh, nz = dims
    ny, nxc = nyl * nyh, nx * nc

    def per_device(embeddings, second_view, prototypes, row_scale, col_scale):
        row_count, width = embeddings.shape
        proto_count = prototypes.shape[0]
        proto_total = proto_count * nx * nyl * nc
        rows, cols = row_count * nyh, proto_count // nyh
        per_block = row_count // LANES
        chunks, groups = rows // LANES, cols // LANES
        rows_out, cols_out = row_count // (nx * nyl * nc), cols // nz
        dma = pltpu.SemaphoreType.DMA
        scratch = [
            pltpu.VMEM((2, chunks, LANES, width), BF16),
            pltpu.VMEM((cols, width), BF16),
            pltpu.VMEM((chunks, 1, LANES), F32),
            pltpu.VMEM((groups, LANES), F32),
            pltpu.VMEM((rows, cols), F32),
            pltpu.VMEM((rows, cols), F32),
            pltpu.VMEM((LANES, cols), F32),
            pltpu.VMEM((rows, cols), BF16),
            pltpu.VMEM((rows, cols), BF16),
            pltpu.VMEM((cols, width), F32),
            pltpu.VMEM((groups, 8, LANES), F32),
            pltpu.VMEM((groups, 8, LANES), F32),
            pltpu.VMEM((nxc, 2, chunks, LANES), F32),
            pltpu.VMEM((ny, 2, chunks, LANES), F32),
            pltpu.VMEM((nz, 2, groups, LANES), F32),
            pltpu.VMEM((ITERS, nxc, chunks, LANES), F32),
            pltpu.VMEM((ITERS, ny, chunks, LANES), F32),
            pltpu.VMEM((ITERS, nz, groups, LANES), F32),
            pltpu.VMEM((nyh, nx, nyl, nc * rows_out, width), BF16),
            pltpu.VMEM((ny, nx, nc * rows_out, width), BF16),
            pltpu.VMEM((nxc, rows_out, width), F32),
            pltpu.VMEM((nxc, rows_out, width), F32),
            pltpu.VMEM((nz, cols_out, width), BF16),
            pltpu.VMEM((nz, cols_out, width), BF16),
            dma((5,)),
            dma((nyh,)),
            dma((nyh,)),
            dma((nyh,)),
            dma((nyh,)),
            dma((nyh,)),
            dma((nyh,)),
            dma((nxc,)),
            dma((ny,)),
            dma((nz,)),
            dma((nz,)),
            dma((ITERS, nxc)),
            dma((ITERS, ny)),
            dma((ITERS + 1, nz)),
            dma((nxc,)),
            dma((ny,)),
            dma((nz,)),
            dma((nxc,)),
            dma((ny,)),
            dma((nz,)),
        ]
        return pl.pallas_call(
            functools.partial(kernel, dims, proto_total),
            out_shape=(
                jax.ShapeDtypeStruct((rows_out, width), F32),
                jax.ShapeDtypeStruct((cols_out, width), F32),
            ),
            in_specs=[pl.BlockSpec(memory_space=pl.ANY)] * 5,
            out_specs=(pl.BlockSpec(memory_space=pltpu.VMEM),) * 2,
            scratch_shapes=scratch,
            compiler_params=pltpu.CompilerParams(
                collective_id=0, has_side_effects=True, vmem_limit_bytes=48 * 1024 * 1024
            ),
        )(
            embeddings.reshape(per_block, LANES, width),
            second_view.reshape(per_block, LANES, width),
            prototypes.reshape(nyh, cols, width),
            row_scale.reshape(per_block, 1, LANES),
            col_scale.reshape(nyh, groups, LANES),
        )

    return jax.shard_map(
        per_device,
        mesh=mesh,
        in_specs=(P("row", None), P("row", None), P("proto", None), P("row"), P("proto")),
        out_specs=(P(("row", "proto"), None), P(("proto", "row"), None)),
        check_vma=False,
    )


def solution(mesh):
    return build(mesh, DIMS)
```

time: 1080 us -> 105 us (0.10)
  blocking collectives: 705 us -> 0 us
  waiting for transfers between devices: 309 us -> 0 us
  Pallas kernels: 0 us -> 98.2 us
  matrix products: 44.6 us -> 0 us
  between operations: 14.1 us -> 0.65 us
    psum x8 -> x0, blocking collectives: 705 us -> none  [the longest x3 373 us: solve_cols(): lax.psum(jnp.dot(duals_rows, plan_now(), precision=lax.Precision.HIGHEST)...]
    reduce_scatter x2 -> x0, waiting for transfers between devices: 309 us -> none  [the longest x1 230 us: per_device(): lax.psum_scatter(contract_rows(stacked, sources), 'row', scatter_dimensio...]
    pallas_call x0 -> x1, Pallas kernels: none -> 98.2 us  [per_device(): pl.pallas_call(functools.partial(kernel, dims, proto_total), out_shape=(j...]
    dot_general x11 -> x0, matrix products: 44.6 us -> none  [the longest x4 17.4 us: solve_cols(): jnp.dot(duals_rows, plan_now(), precision=lax.Precision.HIGHEST)]
  transfers between devices with their start and end apart: 2 -> 0, of which waited for: 2 -> 0; matrix products, arithmetic and copies ran while one was open for 0% -> 0% of each run, Pallas kernels for 0% -> 0%
where the time goes in v1:
time: 105 us; the launch traced here: 104 us
  Pallas kernels  98.2 us (94%)
  local copies, waits for them, and re-layouts  5.52 us (5%)
    pallas_call x1, Pallas kernels, per_device(): pl.pallas_call(functools.partial(kernel, dims, proto_total), out_shape=(j...  98.2 us
    unnamed x12, local copies, waits for them, and re-layouts  5.52 us

profile of v1, /device:TPU:1, one launch (start us, length us, event | category | flops | bytes accessed | tf_op | source)
XLA Modules:
  0.0 104.4 jit_solution(8046523445558675213)
XLA Ops:
  0.6 0.0 copy-start.4
  0.6 0.7 copy-done.4
  1.3 0.0 copy-start
  1.3 1.2 %copy-done = bf16[4096,128]{1,0:T(8,128)(2,1)S(1)} copy-done((bf16[4096,128]{1,0:T(8,128)(2,1)S(1)}, bf16[4096,128]{1,0:T(8,128)(2,1)}, u32[]{:S(2)}) %copy-start) | copy-done | bytes 1048600
  2.5 0.0 copy-start.1
  2.5 0.8 copy-done.1
  3.4 0.0 copy-start.2
  3.4 0.8 copy-done.2
  4.2 0.0 copy-start.3
  4.2 0.7 copy-done.3
  4.9 98.2 %shard_map.68 = (f32[16,128]{1,0:T(8,128)S(1)}, f32[128,128]{1,0:T(8,128)S(1)}) custom-call(bf16[2,128,128]{2,1,0:T(8,128)(2,1)S(1)} %bitcast.6, bf16[2,128,128]{2,1,0:T(8,128)(2,1)S(1)} %bitcast.7, bf16[4,1024,128]{2,1,0:T(8,128)(2,1)S(1)} %bitcast.5, f32[2,1,128]{2,1,0:T(1,128)S(1)} %bitcast.9, f32[4,8,128]{2,1,0:T(8,128)S(1)} %bitcast.8), custom_call_target="tpu_custom_call" | custom-call | tf_op jit(solution)/shard_map/pallas_call | solution.py:463
  103.2 0.6 copy.9
  103.8 0.6 copy.10
Async XLA Ops:
  0.6 0.7 copy-start.4
  1.3 1.2 %copy-start = (bf16[4096,128]{1,0:T(8,128)(2,1)S(1)}, bf16[4096,128]{1,0:T(8,128)(2,1)}, u32[]{:S(2)}) copy-start(bf16[4096,128]{1,0:T(8,128)(2,1)} %param.7) | copy-start | bytes 3145732
  2.5 0.8 copy-start.1
  3.4 0.8 copy-start.2
  4.2 0.7 copy-start.3

commit v2 on v0

v2 whole, which is shorter than its diff:
```python
import functools
from types import SimpleNamespace

import jax
import jax.numpy as jnp
from jax import lax
from jax.experimental import pallas as pl
from jax.experimental.pallas import tpu as pltpu
from jax.sharding import PartitionSpec as P

ITERS = 4
LANES = 128
MESH = pl.DeviceIdType.MESH
F32 = jnp.float32
BF16 = jnp.bfloat16

DIMS = (4, 2, 2, 4, 8)


def dot_nt(left, right):
    return lax.dot_general(left, right, (((1,), (1,)), ((), ())), preferred_element_type=F32)


def dot_tn(left, right):
    return lax.dot_general(left, right, (((0,), (0,)), ((), ())), preferred_element_type=F32)


def down(row):
    return jnp.broadcast_to(row, (LANES, LANES)).T


def fold(block):
    return block.reshape(block.shape[0] // 8, 8, LANES).sum(0)


def across(block):
    return block.T.sum(0, keepdims=True)


def tiles_of(count, start=0):
    return [slice((start + g) * LANES, (start + g + 1) * LANES) for g in range(count)]


def aligned(i, size=LANES):
    return pl.ds(pl.multiple_of(i * size, size), size)


def kernel(dims, proto_total, names, emb_in, view_in, pro_in, rs_in, cs_in, eg_ref, pg_ref, *scratch):
    m = SimpleNamespace(**dict(zip(names, scratch)))
    nx, nyl, nc, nyh, nz = dims
    ny, nxc, npr = nyl * nyh, nx * nc, nx * nyl * nc
    row_id, me_p = lax.axis_index("row"), lax.axis_index("proto")
    yh, z = row_id // nz, row_id % nz
    core = me_p % nc
    yl = (me_p // nc) % nyl
    x = me_p // (nc * nyl)
    y = yh * nyl + yl
    xc = x * nc + core

    def at_z(other):
        return (yh * nz + other, me_p)

    def at_yh(other):
        return (other * nz + z, me_p)

    def at_y(other):
        return ((other // nyl) * nz + z, (x * nyl + other % nyl) * nc + core)

    def at_xc(other):
        return (row_id, ((other // nc) * nyl + yl) * nc + other % nc)

    def at_p(other):
        return (row_id, other)

    chunks, groups = m.plan.shape[0] // LANES, m.plan.shape[1] // LANES
    per_block = chunks // nyh
    width = emb_in.shape[-1]
    logit_scale = 1.0 / (0.05 * width)
    view_scale = 1.0 / (0.1 * width)
    mass_inverse = 1.0 / (64.0 * proto_total)

    own = pl.ds(yh * per_block, per_block)
    small_loads = [
        pltpu.make_async_copy(emb_in, m.ev.at[0, own], m.local_sem.at[0]),
        pltpu.make_async_copy(view_in, m.ev.at[1, own], m.local_sem.at[1]),
        pltpu.make_async_copy(rs_in, m.rs.at[own], m.local_sem.at[2]),
        pltpu.make_async_copy(cs_in, m.cs, m.local_sem.at[3]),
    ]
    for load in small_loads:
        load.start()

    def pro_load(part):
        return pltpu.make_async_copy(pro_in.at[part], m.pr.at[part], m.pro_sem.at[part])

    for part in range(nyh):
        pro_load(part).start()

    barrier = pltpu.get_barrier_semaphore()
    for count, me, address in ((nz, z, at_z), (ny, y, at_y), (npr, me_p, at_p)):
        for step in range(1, count):
            pl.semaphore_signal(
                barrier, inc=1, device_id=address((me + step) % count), device_id_type=MESH
            )
    for load in small_loads:
        load.wait()

    m.colm[...] = jnp.zeros_like(m.colm)
    m.colw[...] = jnp.zeros_like(m.colw)
    m.rowm[...] = jnp.zeros_like(m.rowm)
    m.roww[...] = jnp.zeros_like(m.roww)

    def own_part(part, h):
        i = yh * per_block + h
        rows = aligned(h)
        m.lg[...] = dot_nt(m.ev[0, i], m.pr[part])
        m.cot0[part, rows, :] = dot_nt(m.ev[1, i], m.pr[part]) * -view_scale
        scale = down(m.rs[i]) * mass_inverse
        mass = m.rowm[h]
        weight = m.roww[h]
        for g, cols in enumerate(tiles_of(groups)):
            value = scale * m.cs[part, g : g + 1, :] * jnp.exp(m.lg[:, cols] * logit_scale)
            m.plan0[part, rows, cols] = value
            weighted = value * m.cot0[part, rows, cols]
            mass = mass + value
            weight = weight + weighted
            m.colm[part, g] += fold(value)
            m.colw[part, g] += fold(weighted)
        m.rowm[h] = mass
        m.roww[h] = weight

    def own_parts(first, last):
        @pl.loop(first, last)
        def _(part):
            pro_load(part).wait()

            @pl.loop(0, per_block)
            def _(h):
                own_part(part, h)

    own_parts(0, nyh // 2)
    pl.semaphore_wait(barrier, nz + ny + npr - 3)

    sign = 2 * yl - 1
    partner = at_xc(x * nc + (core + 1) % nc)
    blocks = []
    sends = []
    for step in range(1, nyh):
        target = (y + sign * step + ny) % ny
        source = (y + (sign if step % 2 else -sign) * step + ny) % ny
        blocks.append((source // nyl, pl.ds((source // nyl) * per_block, per_block)))
        rows_out = pltpu.make_async_remote_copy(
            m.ev.at[core, own], m.ev.at[core, own], m.g_send.at[step], m.g_recv.at[step], at_y(target), MESH
        )
        scale_out = pltpu.make_async_remote_copy(
            m.rs.at[own], m.rs.at[own], m.r_send.at[step], m.r_recv.at[step], at_y(target), MESH
        )
        rows_out.start()
        scale_out.start()
        sends += [rows_out, scale_out]

    own_parts(nyh // 2, nyh)

    def start(slots, me, count, address, send, recv):
        for step in range(1, count):
            other = (me + step) % count
            pltpu.make_async_remote_copy(
                slots.at[me], slots.at[me], send.at[step], recv.at[me], address(other), MESH
            ).start()

    def finish(slots, me, count, address, send, recv):
        for step in range(1, count):
            other = (me + step) % count
            pltpu.make_async_remote_copy(
                slots.at[other], slots.at[other], send.at[step], recv.at[other], address(other), MESH
            ).wait_recv()
        for step in range(1, count):
            other = (me + step) % count
            pltpu.make_async_remote_copy(
                slots.at[me], slots.at[me], send.at[step], recv.at[me], address(other), MESH
            ).wait_send()

    def scatter(shares, slots, me, count, address, send, recv):
        copies = []
        for step in range(1, count):
            other = (me + step) % count
            copies.append(
                pltpu.make_async_remote_copy(
                    shares.at[other], slots.at[me], send.at[step], recv.at[me], address(other), MESH
                )
            )
            copies[-1].start()
        return copies

    def arrived(slots, me, count, address, send, recv):
        for step in range(1, count):
            other = (me + step) % count
            pltpu.make_async_remote_copy(
                slots.at[other], slots.at[other], send.at[step], recv.at[other], address(other), MESH
            ).wait_recv()

    def total(slots, count):
        result = slots[0]
        for slot in range(1, count):
            result = result + slots[slot]
        return result

    along_x = (xc, nxc, at_xc)
    along_y = (y, ny, at_y)
    along_z = (z, nz, at_z)
    along_p = (me_p, npr, at_p)
    along_h = (yh, nyh, at_yh)

    for h in range(per_block):
        m.bw[me_p, h : h + 1, :] = across(m.rowm[h])
        m.bw[me_p, per_block + h : per_block + h + 1, :] = across(m.roww[h])
    start(m.bw, *along_p, m.w_send, m.w_recv)

    own_rows = aligned(yh, per_block * LANES)
    moves = [
        pltpu.make_async_copy(m.plan0.at[yh], m.plan.at[own_rows], m.local_sem.at[0]),
        pltpu.make_async_copy(m.cot0.at[yh], m.cot.at[own_rows], m.local_sem.at[1]),
    ]
    for move in moves:
        move.start()

    for part in range(nyh):
        for g in range(groups):
            m.cms[part, 0, g : g + 1, :] = m.colm[part, g].sum(0, keepdims=True)
            m.cms[part, 1, g : g + 1, :] = m.colw[part, g].sum(0, keepdims=True)
    sends += scatter(m.cms, m.cmr, *along_h, m.cm_send, m.cm_recv)
    m.cmr[yh] = m.cms[yh]

    finish(m.bw, *along_p, m.w_send, m.w_recv)
    sums = total(m.bw, npr)
    m.rsum[yh] = sums
    m.dual0[...] = sums[per_block:] / sums[:per_block]
    start(m.rsum, *along_h, m.q_send, m.q_recv)

    @pl.loop(0, nyh)
    def _(part):
        found = [jnp.zeros((8, LANES), F32)] * groups
        for h in range(per_block):
            dual = down(m.dual0[h : h + 1, :])
            for g, cols in enumerate(tiles_of(groups)):
                found[g] = found[g] + fold(m.plan0[part, h * LANES : (h + 1) * LANES, cols] * dual)
        for g in range(groups):
            m.cps[part, g : g + 1, :] = found[g].sum(0, keepdims=True)

    sends += scatter(m.cps, m.cpr, *along_h, m.cp_send, m.cp_recv)
    m.cpr[yh] = m.cps[yh]

    for step, (block, there) in enumerate(blocks, 1):
        mine = m.ev.at[core, there]
        pltpu.make_async_remote_copy(
            mine, mine, m.g_send.at[step], m.g_recv.at[step], partner, MESH
        ).wait_recv()
        hand = pltpu.make_async_remote_copy(
            mine, mine, m.c_send.at[step], m.c_recv.at[step], partner, MESH
        )
        hand.start()
        sends.append(hand)

    arrived(m.cmr, *along_h, m.cm_send, m.cm_recv)
    m.bz0[z] = total(m.cmr, nyh)
    start(m.bz0, *along_z, m.z0_send, m.z_recv.at[0])

    def fill(step):
        block, there = blocks[step - 1]
        taken = m.ev.at[(core + 1) % nc, there]
        scales = m.rs.at[there]
        pltpu.make_async_remote_copy(
            scales, scales, m.r_send.at[step], m.r_recv.at[step], partner, MESH
        ).wait_recv()
        pltpu.make_async_remote_copy(
            taken, taken, m.c_send.at[step], m.c_recv.at[step], partner, MESH
        ).wait_recv()

        @pl.loop(0, per_block)
        def _(h):
            i = block * per_block + h
            rows = aligned(i)
            m.lg[...] = dot_nt(m.ev[0, i], m.pr[yh])
            m.cot[rows, :] = dot_nt(m.ev[1, i], m.pr[yh]) * -view_scale
            scale = down(m.rs[i]) * mass_inverse
            for g, cols in enumerate(tiles_of(groups)):
                m.plan[rows, cols] = (
                    scale * m.cs[yh, g : g + 1, :] * jnp.exp(m.lg[:, cols] * logit_scale)
                )

    fill(1)
    arrived(m.cpr, *along_h, m.cp_send, m.cp_recv)
    m.bz[ITERS - 1, z] = total(m.cpr, nyh)
    start(m.bz.at[ITERS - 1], *along_z, m.z_send, m.z_recv.at[ITERS])
    for step in range(2, nyh):
        fill(step)
    finish(m.rsum, *along_h, m.q_send, m.q_recv)
    for block in range(nyh):
        place = slice(block * per_block, (block + 1) * per_block)
        m.row_mass[place, :] = m.rsum[block, :per_block, :]
        m.row_weight[place, :] = m.rsum[block, per_block:, :]
    for move in moves:
        move.wait()
    finish(m.bz0, *along_z, m.z0_send, m.z_recv.at[0])
    col_sums = total(m.bz0, nz)
    col_mass, col_weight = col_sums[0], col_sums[1]
    finish(m.bz.at[ITERS - 1], *along_z, m.z_send, m.z_recv.at[ITERS])
    col_dual = (col_weight - total(m.bz.at[ITERS - 1], nz)) / col_mass

    def column_part(row_dual, k):
        m.bx[k, xc] = row_dual
        found = tuple(jnp.zeros((8, LANES), F32) for _ in range(groups))

        def add(i, found):
            rows = aligned(i)
            dual = down(m.bx[k, xc, pl.ds(i, 1), :])
            return tuple(
                tile + fold(m.plan[rows, cols] * dual)
                for tile, cols in zip(found, tiles_of(groups))
            )

        found = lax.fori_loop(0, chunks, add, found)
        for g, tile in enumerate(found):
            m.bz[k, z, g : g + 1, :] = tile.sum(0, keepdims=True)

    def row_part(col_dual, k):
        @pl.loop(0, chunks)
        def _(i):
            rows = aligned(i)
            block = m.plan[rows, :LANES] * col_dual[0:1, :]
            for g, cols in enumerate(tiles_of(groups - 1, 1), 1):
                block = block + m.plan[rows, cols] * col_dual[g : g + 1, :]
            m.bx[k, xc, pl.ds(i, 1), :] = across(block)

    def sweep(k, duals):
        row_part(duals[1], k)
        start(m.bx.at[k], *along_x, m.x_send, m.x_recv.at[k])

        @pl.when(k == 0)
        def _():
            @pl.loop(0, chunks)
            def _(i):
                rows = aligned(i)
                m.splan[rows, :] = (m.plan[rows, :] * -view_scale).astype(BF16)

        finish(m.bx.at[k], *along_x, m.x_send, m.x_recv.at[k])
        m.by[k, y] = total(m.bx.at[k], nxc)
        start(m.by.at[k], *along_y, m.y_send, m.y_recv.at[k])

        @pl.when(k == 0)
        def _():
            @pl.loop(0, groups)
            def _(g):
                cols = aligned(g)
                m.tail[cols, :] = dot_tn(m.splan[:, cols], m.ev[1].reshape(chunks * LANES, width))

        finish(m.by.at[k], *along_y, m.y_send, m.y_recv.at[k])
        row_dual = (m.row_weight[...] - total(m.by.at[k], ny)) / m.row_mass[...]
        column_part(row_dual, k)
        start(m.bz.at[k], *along_z, m.z_send, m.z_recv.at[k + 1])
        finish(m.bz.at[k], *along_z, m.z_send, m.z_recv.at[k + 1])
        return row_dual, (col_weight - total(m.bz.at[k], nz)) / col_mass

    row_dual, col_dual = lax.fori_loop(
        0, ITERS - 1, sweep, (jnp.zeros((chunks, LANES), F32), col_dual)
    )

    m.bx[0, xc] = row_dual
    half = nx // per_block

    def last_chunk(block, h):
        i = block * per_block + h
        rows = aligned(i)
        dual = down(m.bx[0, xc, pl.ds(i, 1), :])
        for g, cols in enumerate(tiles_of(groups)):
            piece = m.plan[rows, cols] * (m.cot[rows, cols] - dual - col_dual[g : g + 1, :])
            m.grad[rows, cols] = (logit_scale * piece).astype(BF16)
        product = jnp.dot(m.grad[rows, :], m.pr[yh], preferred_element_type=F32)
        m.eb[block, pl.ds(h * half, half)] = product.reshape(
            half, nyl, nc, LANES // (half * nyl * nc), width
        ).astype(BF16)

    for step in range(1, nyh + 1):
        block = (yh + step) % nyh

        @pl.loop(0, per_block)
        def _(h):
            last_chunk(block, h)

        for turn in range(1, nxc):
            other = (xc + turn) % nxc
            sends.append(
                pltpu.make_async_remote_copy(
                    m.eb.at[block, other // nc, :, other % nc],
                    m.fx.at[block, xc],
                    m.fx_send.at[step - 1, turn],
                    m.fx_recv.at[block, xc],
                    at_xc(other),
                    MESH,
                )
            )
            sends[-1].start()

    for step in range(1, nz + 1):
        other = (z + step) % nz
        cols = aligned(other)
        share = m.tail[cols, :] + dot_tn(m.grad[:, cols], m.ev[0].reshape(chunks * LANES, width))
        if step < nz:
            m.pb[step] = share.astype(BF16)
            sends.append(
                pltpu.make_async_remote_copy(
                    m.pb.at[step], m.fz.at[z], m.fz_send.at[step], m.fz_recv.at[z], at_z(other), MESH
                )
            )
            sends[-1].start()
        else:
            pg_ref[...] = share

    for step in range(1, nyh + 1):
        block = (yh + step) % nyh
        arrived(m.fx.at[block], *along_x, m.fx_send.at[step - 1], m.fx_recv.at[block])
        part = m.eb[block, x, :, core].astype(F32)
        for turn in range(1, nxc):
            part = part + m.fx[block, (xc + turn) % nxc].astype(F32)
        m.fy_out[pl.ds(block * nyl, nyl)] = part
        for low in range(nyl):
            if step < nyh:
                other, slot = block * nyl + low, (step - 1) * nyl + low
            elif low:
                other, slot = yh * nyl + (yl + low) % nyl, (step - 1) * nyl + low
            else:
                continue
            sends.append(
                pltpu.make_async_remote_copy(
                    m.fy_out.at[other], m.fy.at[y], m.fy_send.at[slot], m.fy_recv.at[y], at_y(other), MESH
                )
            )
            sends[-1].start()

    arrived(m.fz, *along_z, m.fz_send, m.fz_recv)
    share = pg_ref[...]
    for step in range(1, nz):
        share = share + m.fz[(z + step) % nz].astype(F32)
    pg_ref[...] = share

    arrived(m.fy, *along_y, m.fy_send, m.fy_recv)
    rows_out = m.fy_out[y]
    for step in range(1, ny):
        rows_out = rows_out + m.fy[(y + step) % ny]
    eg_ref[...] = rows_out

    for send in sends:
        send.wait_send()


def build(mesh, dims):
    nx, nyl, nc, nyh, nz = dims
    ny, nxc, npr = nyl * nyh, nx * nc, nx * nyl * nc

    def per_device(embeddings, second_view, prototypes, row_scale, col_scale):
        row_count, width = embeddings.shape
        proto_count = prototypes.shape[0]
        proto_total = proto_count * npr
        rows, cols = row_count * nyh, proto_count // nyh
        per_block = row_count // LANES
        chunks, groups = rows // LANES, cols // LANES
        rows_out, cols_out = row_count // npr, cols // nz
        vmem, dma = pltpu.VMEM, pltpu.SemaphoreType.DMA
        scratch = dict(
            ev=vmem((2, chunks, LANES, width), BF16),
            pr=vmem((nyh, cols, width), BF16),
            rs=vmem((chunks, 1, LANES), F32),
            cs=vmem((nyh, groups, LANES), F32),
            plan0=vmem((nyh, row_count, cols), F32),
            cot0=vmem((nyh, row_count, cols), F32),
            plan=vmem((rows, cols), F32),
            cot=vmem((rows, cols), F32),
            lg=vmem((LANES, cols), F32),
            grad=vmem((rows, cols), BF16),
            splan=vmem((rows, cols), BF16),
            tail=vmem((cols, width), F32),
            colm=vmem((nyh, groups, 8, LANES), F32),
            colw=vmem((nyh, groups, 8, LANES), F32),
            rowm=vmem((per_block, LANES, LANES), F32),
            roww=vmem((per_block, LANES, LANES), F32),
            bw=vmem((npr, 2 * per_block, LANES), F32),
            rsum=vmem((nyh, 2 * per_block, LANES), F32),
            dual0=vmem((per_block, LANES), F32),
            row_mass=vmem((chunks, LANES), F32),
            row_weight=vmem((chunks, LANES), F32),
            cms=vmem((nyh, 2, groups, LANES), F32),
            cmr=vmem((nyh, 2, groups, LANES), F32),
            cps=vmem((nyh, groups, LANES), F32),
            cpr=vmem((nyh, groups, LANES), F32),
            bz0=vmem((nz, 2, groups, LANES), F32),
            bx=vmem((ITERS - 1, nxc, chunks, LANES), F32),
            by=vmem((ITERS - 1, ny, chunks, LANES), F32),
            bz=vmem((ITERS, nz, groups, LANES), F32),
            eb=vmem((nyh, nx, nyl, nc, rows_out, width), BF16),
            fx=vmem((nyh, nxc, nyl, rows_out, width), BF16),
            fy_out=vmem((ny, rows_out, width), F32),
            fy=vmem((ny, rows_out, width), F32),
            pb=vmem((nz, cols_out, width), BF16),
            fz=vmem((nz, cols_out, width), BF16),
            local_sem=dma((4,)),
            pro_sem=dma((nyh,)),
            g_send=dma((nyh,)),
            g_recv=dma((nyh,)),
            r_send=dma((nyh,)),
            r_recv=dma((nyh,)),
            c_send=dma((nyh,)),
            c_recv=dma((nyh,)),
            w_send=dma((npr,)),
            w_recv=dma((npr,)),
            q_send=dma((nyh,)),
            q_recv=dma((nyh,)),
            cm_send=dma((nyh,)),
            cm_recv=dma((nyh,)),
            cp_send=dma((nyh,)),
            cp_recv=dma((nyh,)),
            x_send=dma((nxc,)),
            y_send=dma((ny,)),
            z_send=dma((nz,)),
            z0_send=dma((nz,)),
            x_recv=dma((ITERS - 1, nxc)),
            y_recv=dma((ITERS - 1, ny)),
            z_recv=dma((ITERS + 1, nz)),
            fx_send=dma((nyh, nxc)),
            fx_recv=dma((nyh, nxc)),
            fy_send=dma((ny,)),
            fy_recv=dma((ny,)),
            fz_send=dma((nz,)),
            fz_recv=dma((nz,)),
        )
        return pl.pallas_call(
            functools.partial(kernel, dims, proto_total, tuple(scratch)),
            out_shape=(
                jax.ShapeDtypeStruct((rows_out, width), F32),
                jax.ShapeDtypeStruct((cols_out, width), F32),
            ),
            in_specs=[pl.BlockSpec(memory_space=pltpu.HBM)] * 5,
            out_specs=(pl.BlockSpec(memory_space=pltpu.VMEM),) * 2,
            scratch_shapes=list(scratch.values()),
            compiler_params=pltpu.CompilerParams(
                collective_id=0, has_side_effects=True, vmem_limit_bytes=60 * 1024 * 1024
            ),
        )(
            embeddings.reshape(per_block, LANES, width),
            second_view.reshape(per_block, LANES, width),
            prototypes.reshape(nyh, cols, width),
            row_scale.reshape(per_block, 1, LANES),
            col_scale.reshape(nyh, groups, LANES),
        )

    return jax.shard_map(
        per_device,
        mesh=mesh,
        in_specs=(P("row", None), P("row", None), P("proto", None), P("row"), P("proto")),
        out_specs=(P(("row", "proto"), None), P(("proto", "row"), None)),
        check_vma=False,
    )


def solution(mesh):
    return build(mesh, DIMS)
```

time: 1080 us -> 92 us (0.09)
  blocking collectives: 705 us -> 0 us
  waiting for transfers between devices: 309 us -> 0 us
  Pallas kernels: 0 us -> 87.9 us
  matrix products: 44.6 us -> 0 us
  between operations: 14.1 us -> 0.64 us
    psum x8 -> x0, blocking collectives: 705 us -> none  [the longest x3 373 us: solve_cols(): lax.psum(jnp.dot(duals_rows, plan_now(), precision=lax.Precision.HIGHEST)...]
    reduce_scatter x2 -> x0, waiting for transfers between devices: 309 us -> none  [the longest x1 230 us: per_device(): lax.psum_scatter(contract_rows(stacked, sources), 'row', scatter_dimensio...]
    pallas_call x0 -> x1, Pallas kernels: none -> 87.9 us  [per_device(): pl.pallas_call(functools.partial(kernel, dims, proto_total, tuple(scratch...]
    dot_general x11 -> x0, matrix products: 44.6 us -> none  [the longest x4 17.4 us: solve_cols(): jnp.dot(duals_rows, plan_now(), precision=lax.Precision.HIGHEST)]
  transfers between devices with their start and end apart: 2 -> 0, of which waited for: 2 -> 0; matrix products, arithmetic and copies ran while one was open for 0% -> 0% of each run, Pallas kernels for 0% -> 0%
where the time goes in v2:
time: 92 us; the launch traced here: 91.3 us
  Pallas kernels  87.9 us (96%)
  local copies, waits for them, and re-layouts  2.77 us (3%)
    pallas_call x1, Pallas kernels, per_device(): pl.pallas_call(functools.partial(kernel, dims, proto_total, tuple(scratch...  87.9 us
    unnamed x2, local copies, waits for them, and re-layouts  2.77 us

profile of v2, /device:TPU:1, one launch (start us, length us, event | category | flops | bytes accessed | tf_op | source)
XLA Modules:
  0.0 91.3 jit_solution(13053374461509273088)
XLA Ops:
  0.6 87.9 %shard_map.68 = (f32[16,128]{1,0:T(8,128)}, f32[128,128]{1,0:T(8,128)}) custom-call(bf16[2,128,128]{2,1,0:T(8,128)(2,1)} %bitcast.6, bf16[2,128,128]{2,1,0:T(8,128)(2,1)} %bitcast.7, bf16[4,1024,128]{2,1,0:T(8,128)(2,1)} %bitcast.5, f32[2,1,128]{2,1,0:T(1,128)} %bitcast.9, f32[4,8,128]{2,1,0:T(8,128)} %bitcast.8), custom_call_target="tpu_custom_call" | custom-call | tf_op jit(solution)/shard_map/pallas_call | solution.py:534
  88.5 1.3 %copy.9 = f32[16,128]{1,0:T(8,128)} copy(f32[16,128]{1,0:T(8,128)} %get-tuple-element.4) | data formatting | bytes 16384
  89.8 1.5 %copy.10 = f32[128,128]{1,0:T(8,128)} copy(f32[128,128]{1,0:T(8,128)} %get-tuple-element.5) | data formatting | bytes 131072

commit v3 on v2

--- a/solution.py
+++ b/solution.py
@@ -1,4 +1,5 @@
 import functools
+import math
 from types import SimpleNamespace
 
 import jax
@@ -78,6 +79,7 @@
     logit_scale = 1.0 / (0.05 * width)
     view_scale = 1.0 / (0.1 * width)
     mass_inverse = 1.0 / (64.0 * proto_total)
+    exp2_scale = logit_scale * math.log2(math.e)
 
     own = pl.ds(yh * per_block, per_block)
     small_loads = [
@@ -104,38 +106,41 @@
     for load in small_loads:
         load.wait()
 
-    m.colm[...] = jnp.zeros_like(m.colm)
-    m.colw[...] = jnp.zeros_like(m.colw)
     m.rowm[...] = jnp.zeros_like(m.rowm)
     m.roww[...] = jnp.zeros_like(m.roww)
 
-    def own_part(part, h):
-        i = yh * per_block + h
-        rows = aligned(h)
-        m.lg[...] = dot_nt(m.ev[0, i], m.pr[part])
-        m.cot0[part, rows, :] = dot_nt(m.ev[1, i], m.pr[part]) * -view_scale
-        scale = down(m.rs[i]) * mass_inverse
-        mass = m.rowm[h]
-        weight = m.roww[h]
-        for g, cols in enumerate(tiles_of(groups)):
-            value = scale * m.cs[part, g : g + 1, :] * jnp.exp(m.lg[:, cols] * logit_scale)
-            m.plan0[part, rows, cols] = value
-            weighted = value * m.cot0[part, rows, cols]
-            mass = mass + value
-            weight = weight + weighted
-            m.colm[part, g] += fold(value)
-            m.colw[part, g] += fold(weighted)
-        m.rowm[h] = mass
-        m.roww[h] = weight
+    def own_part(part):
+        for h in range(per_block):
+            rows = slice(h * LANES, (h + 1) * LANES)
+            scale = down(m.rs[yh * per_block + h]) * mass_inverse
+            mass = m.rowm[h]
+            weight = m.roww[h]
+            for g, cols in enumerate(tiles_of(groups)):
+                value = scale * m.cs[part, g : g + 1, :] * jnp.exp2(m.lg[part % 2, rows, cols] * exp2_scale)
+                m.plan0[part, rows, cols] = value
+                weighted = value * m.dot0[part, rows, cols]
+                mass = mass + value
+                weight = weight + weighted
+                if h:
+                    m.colm[part, g] += fold(value)
+                    m.colw[part, g] += fold(weighted)
+                else:
+                    m.colm[part, g] = fold(value)
+                    m.colw[part, g] = fold(weighted)
+            m.rowm[h] = mass
+            m.roww[h] = weight
+
+    def block_rows(kind, block):
+        place = pl.ds(block * per_block, per_block)
+        return m.ev[kind, place].reshape(per_block * LANES, width)
 
     def own_parts(first, last):
-        @pl.loop(first, last)
-        def _(part):
+        for part in range(first, last):
             pro_load(part).wait()
-
-            @pl.loop(0, per_block)
-            def _(h):
-                own_part(part, h)
+        for part in range(first, last):
+            m.lg[part % 2] = dot_nt(block_rows(0, yh), m.pr[part])
+            m.dot0[part] = dot_nt(block_rows(1, yh), m.pr[part])
+            own_part(part)
 
     own_parts(0, nyh // 2)
     pl.semaphore_wait(barrier, nz + ny + npr - 3)
@@ -218,7 +223,7 @@
     own_rows = aligned(yh, per_block * LANES)
     moves = [
         pltpu.make_async_copy(m.plan0.at[yh], m.plan.at[own_rows], m.local_sem.at[0]),
-        pltpu.make_async_copy(m.cot0.at[yh], m.cot.at[own_rows], m.local_sem.at[1]),
+        pltpu.make_async_copy(m.dot0.at[yh], m.dot.at[own_rows], m.local_sem.at[1]),
     ]
     for move in moves:
         move.start()
@@ -233,11 +238,10 @@
     finish(m.bw, *along_p, m.w_send, m.w_recv)
     sums = total(m.bw, npr)
     m.rsum[yh] = sums
-    m.dual0[...] = sums[per_block:] / sums[:per_block]
+    m.dual0[...] = sums[per_block:] * -view_scale / sums[:per_block]
     start(m.rsum, *along_h, m.q_send, m.q_recv)
 
-    @pl.loop(0, nyh)
-    def _(part):
+    for part in range(nyh):
         found = [jnp.zeros((8, LANES), F32)] * groups
         for h in range(per_block):
             dual = down(m.dual0[h : h + 1, :])
@@ -275,16 +279,16 @@
             taken, taken, m.c_send.at[step], m.c_recv.at[step], partner, MESH
         ).wait_recv()
 
-        @pl.loop(0, per_block)
-        def _(h):
+        m.lg[step % 2] = dot_nt(block_rows(0, block), m.pr[yh])
+        m.dot[aligned(block, per_block * LANES), :] = dot_nt(block_rows(1, block), m.pr[yh])
+        for h in range(per_block):
             i = block * per_block + h
             rows = aligned(i)
-            m.lg[...] = dot_nt(m.ev[0, i], m.pr[yh])
-            m.cot[rows, :] = dot_nt(m.ev[1, i], m.pr[yh]) * -view_scale
+            part_rows = slice(h * LANES, (h + 1) * LANES)
             scale = down(m.rs[i]) * mass_inverse
             for g, cols in enumerate(tiles_of(groups)):
                 m.plan[rows, cols] = (
-                    scale * m.cs[yh, g : g + 1, :] * jnp.exp(m.lg[:, cols] * logit_scale)
+                    scale * m.cs[yh, g : g + 1, :] * jnp.exp2(m.lg[step % 2, part_rows, cols] * exp2_scale)
                 )
 
     fill(1)
@@ -297,39 +301,31 @@
     for block in range(nyh):
         place = slice(block * per_block, (block + 1) * per_block)
         m.row_mass[place, :] = m.rsum[block, :per_block, :]
-        m.row_weight[place, :] = m.rsum[block, per_block:, :]
+        m.row_weight[place, :] = m.rsum[block, per_block:, :] * -view_scale
     for move in moves:
         move.wait()
     finish(m.bz0, *along_z, m.z0_send, m.z_recv.at[0])
     col_sums = total(m.bz0, nz)
-    col_mass, col_weight = col_sums[0], col_sums[1]
+    col_mass, col_weight = col_sums[0], col_sums[1] * -view_scale
     finish(m.bz.at[ITERS - 1], *along_z, m.z_send, m.z_recv.at[ITERS])
     col_dual = (col_weight - total(m.bz.at[ITERS - 1], nz)) / col_mass
 
     def column_part(row_dual, k):
-        m.bx[k, xc] = row_dual
-        found = tuple(jnp.zeros((8, LANES), F32) for _ in range(groups))
-
-        def add(i, found):
-            rows = aligned(i)
-            dual = down(m.bx[k, xc, pl.ds(i, 1), :])
-            return tuple(
-                tile + fold(m.plan[rows, cols] * dual)
-                for tile, cols in zip(found, tiles_of(groups))
-            )
-
-        found = lax.fori_loop(0, chunks, add, found)
-        for g, tile in enumerate(found):
-            m.bz[k, z, g : g + 1, :] = tile.sum(0, keepdims=True)
+        found = [jnp.zeros((8, LANES), F32)] * groups
+        for i in range(chunks):
+            dual = down(row_dual[i : i + 1, :])
+            for g, cols in enumerate(tiles_of(groups)):
+                found[g] = found[g] + fold(m.plan[i * LANES : (i + 1) * LANES, cols] * dual)
+        for g in range(groups):
+            m.bz[k, z, g : g + 1, :] = found[g].sum(0, keepdims=True)
 
     def row_part(col_dual, k):
-        @pl.loop(0, chunks)
-        def _(i):
-            rows = aligned(i)
+        for i in range(chunks):
+            rows = slice(i * LANES, (i + 1) * LANES)
             block = m.plan[rows, :LANES] * col_dual[0:1, :]
             for g, cols in enumerate(tiles_of(groups - 1, 1), 1):
                 block = block + m.plan[rows, cols] * col_dual[g : g + 1, :]
-            m.bx[k, xc, pl.ds(i, 1), :] = across(block)
+            m.bx[k, xc, i : i + 1, :] = across(block)
 
     def sweep(k, duals):
         row_part(duals[1], k)
@@ -364,7 +360,8 @@
         0, ITERS - 1, sweep, (jnp.zeros((chunks, LANES), F32), col_dual)
     )
 
-    m.bx[0, xc] = row_dual
+    m.bx[0, xc] = row_dual * (1.0 / view_scale)
+    col_scaled = col_dual * (1.0 / view_scale)
     half = nx // per_block
 
     def last_chunk(block, h):
@@ -372,8 +369,8 @@
         rows = aligned(i)
         dual = down(m.bx[0, xc, pl.ds(i, 1), :])
         for g, cols in enumerate(tiles_of(groups)):
-            piece = m.plan[rows, cols] * (m.cot[rows, cols] - dual - col_dual[g : g + 1, :])
-            m.grad[rows, cols] = (logit_scale * piece).astype(BF16)
+            piece = m.plan[rows, cols] * (m.dot[rows, cols] + dual + col_scaled[g : g + 1, :])
+            m.grad[rows, cols] = (-view_scale * logit_scale * piece).astype(BF16)
         product = jnp.dot(m.grad[rows, :], m.pr[yh], preferred_element_type=F32)
         m.eb[block, pl.ds(h * half, half)] = product.reshape(
             half, nyl, nc, LANES // (half * nyl * nc), width
@@ -382,8 +379,7 @@
     for step in range(1, nyh + 1):
         block = (yh + step) % nyh
 
-        @pl.loop(0, per_block)
-        def _(h):
+        for h in range(per_block):
             last_chunk(block, h)
 
         for turn in range(1, nxc):
@@ -471,10 +467,10 @@
             rs=vmem((chunks, 1, LANES), F32),
             cs=vmem((nyh, groups, LANES), F32),
             plan0=vmem((nyh, row_count, cols), F32),
-            cot0=vmem((nyh, row_count, cols), F32),
+            dot0=vmem((nyh, row_count, cols), F32),
             plan=vmem((rows, cols), F32),
-            cot=vmem((rows, cols), F32),
-            lg=vmem((LANES, cols), F32),
+            dot=vmem((rows, cols), F32),
+            lg=vmem((2, row_count, cols), F32),
             grad=vmem((rows, cols), BF16),
             splan=vmem((rows, cols), BF16),
             tail=vmem((cols, width), F32),
@@ -541,14 +537,19 @@
             out_specs=(pl.BlockSpec(memory_space=pltpu.VMEM),) * 2,
             scratch_shapes=list(scratch.values()),
             compiler_params=pltpu.CompilerParams(
-                collective_id=0, has_side_effects=True, vmem_limit_bytes=60 * 1024 * 1024
+                collective_id=0, has_side_effects=True, vmem_limit_bytes=40 * 1024 * 1024
             ),
         )(
-            embeddings.reshape(per_block, LANES, width),
-            second_view.reshape(per_block, LANES, width),
-            prototypes.reshape(nyh, cols, width),
-            row_scale.reshape(per_block, 1, LANES),
-            col_scale.reshape(nyh, groups, LANES),
+            *[
+                pltpu.with_memory_space_constraint(array, pltpu.HBM)
+                for array in (
+                    embeddings.reshape(per_block, LANES, width),
+                    second_view.reshape(per_block, LANES, width),
+                    prototypes.reshape(nyh, cols, width),
+                    row_scale.reshape(per_block, 1, LANES),
+                    col_scale.reshape(nyh, groups, LANES),
+                )
+            ]
         )
 
     return jax.shard_map(

time: 92 us -> 84.9 us (0.923)
  Pallas kernels: 87.9 us -> 82.8 us
  local copies, waits for them, and re-layouts: 2.77 us -> 1.23 us
    pallas_call x1, Pallas kernels: 87.9 us -> 82.8 us  [per_device(): pl.pallas_call(functools.partial(kernel, dims, proto_total, tuple(scratch...]
    unnamed x2, local copies, waits for them, and re-layouts: 2.77 us -> 1.23 us
where the time goes in v3:
time: 84.9 us; the launch traced here: 84.7 us
  Pallas kernels  82.8 us (98%)
  local copies, waits for them, and re-layouts  1.23 us (1%)
    pallas_call x1, Pallas kernels, per_device(): pl.pallas_call(functools.partial(kernel, dims, proto_total, tuple(scratch...  82.8 us

profile of v3, /device:TPU:1, one launch (start us, length us, event | category | flops | bytes accessed | tf_op | source)
XLA Modules:
  0.0 84.7 jit_solution(16134996857664974880)
XLA Ops:
  0.6 82.8 %shard_map.68 = (f32[16,128]{1,0:T(8,128)S(1)}, f32[128,128]{1,0:T(8,128)S(1)}) custom-call(bf16[2,128,128]{2,1,0:T(8,128)(2,1)} %bitcast.6, bf16[2,128,128]{2,1,0:T(8,128)(2,1)} %bitcast.7, bf16[4,1024,128]{2,1,0:T(8,128)(2,1)} %bitcast.5, f32[2,1,128]{2,1,0:T(1,128)} %bitcast.9, f32[4,8,128]{2,1,0:T(8,128)} %bitcast.8), custom_call_target="tpu_custom_call" | custom-call | tf_op jit(solution)/shard_map/pallas_call | solution.py:530
  83.5 0.6 copy.9
  84.1 0.6 copy.10

commit v4 on v3

--- a/solution.py
+++ b/solution.py
@@ -44,6 +44,10 @@
 
 def aligned(i, size=LANES):
     return pl.ds(pl.multiple_of(i * size, size), size)
+
+
+def far_first(count):
+    return sorted(range(1, count), key=lambda step: -min(step, count - step))
 
 
 def kernel(dims, proto_total, names, emb_in, view_in, pro_in, rs_in, cs_in, eg_ref, pg_ref, *scratch):
@@ -143,12 +147,68 @@
             own_part(part)
 
     own_parts(0, nyh // 2)
+    own_parts(nyh // 2, nyh)
+    sends = []
+
+    def start(slots, me, count, address, send, recv):
+        for step in far_first(count):
+            other = (me + step) % count
+            pltpu.make_async_remote_copy(
+                slots.at[me], slots.at[me], send.at[step], recv.at[me], address(other), MESH
+            ).start()
+
+    def finish(slots, me, count, address, send, recv):
+        for step in range(1, count):
+            other = (me + step) % count
+            pltpu.make_async_remote_copy(
+                slots.at[other], slots.at[other], send.at[step], recv.at[other], address(other), MESH
+            ).wait_recv()
+        for step in range(1, count):
+            other = (me + step) % count
+            pltpu.make_async_remote_copy(
+                slots.at[me], slots.at[me], send.at[step], recv.at[me], address(other), MESH
+            ).wait_send()
+
+    def scatter(shares, slots, me, count, address, send, recv):
+        copies = []
+        for step in far_first(count):
+            other = (me + step) % count
+            copies.append(
+                pltpu.make_async_remote_copy(
+                    shares.at[other], slots.at[me], send.at[step], recv.at[me], address(other), MESH
+                )
+            )
+            copies[-1].start()
+        return copies
+
+    def arrived(slots, me, count, address, send, recv):
+        for step in range(1, count):
+            other = (me + step) % count
+            pltpu.make_async_remote_copy(
+                slots.at[other], slots.at[other], send.at[step], recv.at[other], address(other), MESH
+            ).wait_recv()
+
+    def total(slots, count):
+        result = slots[0]
+        for slot in range(1, count):
+            result = result + slots[slot]
+        return result
+
+    along_x = (xc, nxc, at_xc)
+    along_y = (y, ny, at_y)
+    along_z = (z, nz, at_z)
+    along_p = (me_p, npr, at_p)
+    along_h = (yh, nyh, at_yh)
+
+    for h in range(per_block):
+        m.bw[me_p, h : h + 1, :] = across(m.rowm[h])
+        m.bw[me_p, per_block + h : per_block + h + 1, :] = across(m.roww[h])
     pl.semaphore_wait(barrier, nz + ny + npr - 3)
+    start(m.bw, *along_p, m.w_send, m.w_recv)
 
     sign = 2 * yl - 1
     partner = at_xc(x * nc + (core + 1) % nc)
     blocks = []
-    sends = []
     for step in range(1, nyh):
         target = (y + sign * step + ny) % ny
         source = (y + (sign if step % 2 else -sign) * step + ny) % ny
@@ -163,63 +223,6 @@
         scale_out.start()
         sends += [rows_out, scale_out]
 
-    own_parts(nyh // 2, nyh)
-
-    def start(slots, me, count, address, send, recv):
-        for step in range(1, count):
-            other = (me + step) % count
-            pltpu.make_async_remote_copy(
-                slots.at[me], slots.at[me], send.at[step], recv.at[me], address(other), MESH
-            ).start()
-
-    def finish(slots, me, count, address, send, recv):
-        for step in range(1, count):
-            other = (me + step) % count
-            pltpu.make_async_remote_copy(
-                slots.at[other], slots.at[other], send.at[step], recv.at[other], address(other), MESH
-            ).wait_recv()
-        for step in range(1, count):
-            other = (me + step) % count
-            pltpu.make_async_remote_copy(
-                slots.at[me], slots.at[me], send.at[step], recv.at[me], address(other), MESH
-            ).wait_send()
-
-    def scatter(shares, slots, me, count, address, send, recv):
-        copies = []
-        for step in range(1, count):
-            other = (me + step) % count
-            copies.append(
-                pltpu.make_async_remote_copy(
-                    shares.at[other], slots.at[me], send.at[step], recv.at[me], address(other), MESH
-                )
-            )
-            copies[-1].start()
-        return copies
-
-    def arrived(slots, me, count, address, send, recv):
-        for step in range(1, count):
-            other = (me + step) % count
-            pltpu.make_async_remote_copy(
-                slots.at[other], slots.at[other], send.at[step], recv.at[other], address(other), MESH
-            ).wait_recv()
-
-    def total(slots, count):
-        result = slots[0]
-        for slot in range(1, count):
-            result = result + slots[slot]
-        return result
-
-    along_x = (xc, nxc, at_xc)
-    along_y = (y, ny, at_y)
-    along_z = (z, nz, at_z)
-    along_p = (me_p, npr, at_p)
-    along_h = (yh, nyh, at_yh)
-
-    for h in range(per_block):
-        m.bw[me_p, h : h + 1, :] = across(m.rowm[h])
-        m.bw[me_p, per_block + h : per_block + h + 1, :] = across(m.roww[h])
-    start(m.bw, *along_p, m.w_send, m.w_recv)
-
     own_rows = aligned(yh, per_block * LANES)
     moves = [
         pltpu.make_async_copy(m.plan0.at[yh], m.plan.at[own_rows], m.local_sem.at[0]),
@@ -291,11 +294,10 @@
                     scale * m.cs[yh, g : g + 1, :] * jnp.exp2(m.lg[step % 2, part_rows, cols] * exp2_scale)
                 )
 
-    fill(1)
     arrived(m.cpr, *along_h, m.cp_send, m.cp_recv)
     m.bz[ITERS - 1, z] = total(m.cpr, nyh)
     start(m.bz.at[ITERS - 1], *along_z, m.z_send, m.z_recv.at[ITERS])
-    for step in range(2, nyh):
+    for step in range(1, nyh):
         fill(step)
     finish(m.rsum, *along_h, m.q_send, m.q_recv)
     for block in range(nyh):
@@ -395,11 +397,13 @@
                 )
             )
             sends[-1].start()
-
-    for step in range(1, nz + 1):
+        if step < nyh:
+            m.tail[...] += dot_tn(m.grad[aligned(block, per_block * LANES), :], block_rows(0, block))
+
+    for step in far_first(nz) + [nz]:
         other = (z + step) % nz
         cols = aligned(other)
-        share = m.tail[cols, :] + dot_tn(m.grad[:, cols], m.ev[0].reshape(chunks * LANES, width))
+        share = m.tail[cols, :] + dot_tn(m.grad[own_rows, cols], block_rows(0, yh))
         if step < nz:
             m.pb[step] = share.astype(BF16)
             sends.append(

time: 84.9 us -> 83.6 us (0.985)
  Pallas kernels: 82.8 us -> 81.3 us
    pallas_call x1, Pallas kernels: 82.8 us -> 81.3 us  [per_device(): pl.pallas_call(functools.partial(kernel, dims, proto_total, tuple(scratch...]
where the time goes in v4:
time: 83.6 us; the launch traced here: 83.2 us
  Pallas kernels  81.3 us (97%)
  local copies, waits for them, and re-layouts  1.23 us (1%)
    pallas_call x1, Pallas kernels, per_device(): pl.pallas_call(functools.partial(kernel, dims, proto_total, tuple(scratch...  81.3 us

profile of v4, /device:TPU:1, one launch (start us, length us, event | category | flops | bytes accessed | tf_op | source)
XLA Modules:
  0.0 83.2 jit_solution(12363704494177891179)
XLA Ops:
  0.6 81.3 %shard_map.68 = (f32[16,128]{1,0:T(8,128)S(1)}, f32[128,128]{1,0:T(8,128)S(1)}) custom-call(bf16[2,128,128]{2,1,0:T(8,128)(2,1)} %bitcast.6, bf16[2,128,128]{2,1,0:T(8,128)(2,1)} %bitcast.7, bf16[4,1024,128]{2,1,0:T(8,128)(2,1)} %bitcast.5, f32[2,1,128]{2,1,0:T(1,128)} %bitcast.9, f32[4,8,128]{2,1,0:T(8,128)} %bitcast.8), custom_call_target="tpu_custom_call" | custom-call | tf_op jit(solution)/shard_map/pallas_call | solution.py:534
  82.0 0.6 copy.9
  82.6 0.6 copy.10

commit v5 on v4

--- a/solution.py
+++ b/solution.py
@@ -83,6 +83,8 @@
     logit_scale = 1.0 / (0.05 * width)
     view_scale = 1.0 / (0.1 * width)
     mass_inverse = 1.0 / (64.0 * proto_total)
+    view_shift = 2.0 ** math.ceil(-math.log2(view_scale))
+    cot_scale = -view_scale * view_shift
     exp2_scale = logit_scale * math.log2(math.e)
 
     own = pl.ds(yh * per_block, per_block)
@@ -109,6 +111,7 @@
             )
     for load in small_loads:
         load.wait()
+    m.ev[1, own] = (m.ev[1, own].astype(F32) * (1.0 / view_shift)).astype(BF16)
 
     m.rowm[...] = jnp.zeros_like(m.rowm)
     m.roww[...] = jnp.zeros_like(m.roww)
@@ -125,12 +128,6 @@
                 weighted = value * m.dot0[part, rows, cols]
                 mass = mass + value
                 weight = weight + weighted
-                if h:
-                    m.colm[part, g] += fold(value)
-                    m.colw[part, g] += fold(weighted)
-                else:
-                    m.colm[part, g] = fold(value)
-                    m.colw[part, g] = fold(weighted)
             m.rowm[h] = mass
             m.roww[h] = weight
 
@@ -231,17 +228,21 @@
     for move in moves:
         move.start()
 
-    for part in range(nyh):
-        for g in range(groups):
-            m.cms[part, 0, g : g + 1, :] = m.colm[part, g].sum(0, keepdims=True)
-            m.cms[part, 1, g : g + 1, :] = m.colw[part, g].sum(0, keepdims=True)
+    @pl.loop(0, nyh)
+    def _(part):
+        for g, cols in enumerate(tiles_of(groups)):
+            value = m.plan0[part, :, cols]
+            m.cms[part, 0, g : g + 1, :] = fold(value).sum(0, keepdims=True)
+            value = value * m.dot0[part, :, cols]
+            m.cms[part, 1, g : g + 1, :] = fold(value).sum(0, keepdims=True)
+
     sends += scatter(m.cms, m.cmr, *along_h, m.cm_send, m.cm_recv)
     m.cmr[yh] = m.cms[yh]
 
     finish(m.bw, *along_p, m.w_send, m.w_recv)
     sums = total(m.bw, npr)
     m.rsum[yh] = sums
-    m.dual0[...] = sums[per_block:] * -view_scale / sums[:per_block]
+    m.dual0[...] = sums[per_block:] * cot_scale / sums[:per_block]
     start(m.rsum, *along_h, m.q_send, m.q_recv)
 
     for part in range(nyh):
@@ -303,12 +304,12 @@
     for block in range(nyh):
         place = slice(block * per_block, (block + 1) * per_block)
         m.row_mass[place, :] = m.rsum[block, :per_block, :]
-        m.row_weight[place, :] = m.rsum[block, per_block:, :] * -view_scale
+        m.row_weight[place, :] = m.rsum[block, per_block:, :] * cot_scale
     for move in moves:
         move.wait()
     finish(m.bz0, *along_z, m.z0_send, m.z_recv.at[0])
     col_sums = total(m.bz0, nz)
-    col_mass, col_weight = col_sums[0], col_sums[1] * -view_scale
+    col_mass, col_weight = col_sums[0], col_sums[1] * cot_scale
     finish(m.bz.at[ITERS - 1], *along_z, m.z_send, m.z_recv.at[ITERS])
     col_dual = (col_weight - total(m.bz.at[ITERS - 1], nz)) / col_mass
 
@@ -338,7 +339,7 @@
             @pl.loop(0, chunks)
             def _(i):
                 rows = aligned(i)
-                m.splan[rows, :] = (m.plan[rows, :] * -view_scale).astype(BF16)
+                m.splan[rows, :] = (m.plan[rows, :] * cot_scale).astype(BF16)
 
         finish(m.bx.at[k], *along_x, m.x_send, m.x_recv.at[k])
         m.by[k, y] = total(m.bx.at[k], nxc)
@@ -362,8 +363,8 @@
         0, ITERS - 1, sweep, (jnp.zeros((chunks, LANES), F32), col_dual)
     )
 
-    m.bx[0, xc] = row_dual * (1.0 / view_scale)
-    col_scaled = col_dual * (1.0 / view_scale)
+    m.bx[0, xc] = row_dual * (1.0 / cot_scale)
+    col_scaled = col_dual * (1.0 / cot_scale)
     half = nx // per_block
 
     def last_chunk(block, h):
@@ -371,8 +372,8 @@
         rows = aligned(i)
         dual = down(m.bx[0, xc, pl.ds(i, 1), :])
         for g, cols in enumerate(tiles_of(groups)):
-            piece = m.plan[rows, cols] * (m.dot[rows, cols] + dual + col_scaled[g : g + 1, :])
-            m.grad[rows, cols] = (-view_scale * logit_scale * piece).astype(BF16)
+            piece = m.plan[rows, cols] * (m.dot[rows, cols] - dual - col_scaled[g : g + 1, :])
+            m.grad[rows, cols] = (cot_scale * logit_scale * piece).astype(BF16)
         product = jnp.dot(m.grad[rows, :], m.pr[yh], preferred_element_type=F32)
         m.eb[block, pl.ds(h * half, half)] = product.reshape(
             half, nyl, nc, LANES // (half * nyl * nc), width
@@ -478,8 +479,6 @@
             grad=vmem((rows, cols), BF16),
             splan=vmem((rows, cols), BF16),
             tail=vmem((cols, width), F32),
-            colm=vmem((nyh, groups, 8, LANES), F32),
-            colw=vmem((nyh, groups, 8, LANES), F32),
             rowm=vmem((per_block, LANES, LANES), F32),
             roww=vmem((per_block, LANES, LANES), F32),
             bw=vmem((npr, 2 * per_block, LANES), F32),

time: 83.6 us -> 83.6 us (level)
  no operation moved by 1% of the time
where the time goes in v5:
time: 83.6 us; the launch traced here: 83.2 us
  Pallas kernels  81.3 us (97%)
  local copies, waits for them, and re-layouts  1.23 us (1%)
    pallas_call x1, Pallas kernels, per_device(): pl.pallas_call(functools.partial(kernel, dims, proto_total, tuple(scratch...  81.3 us

profile of v5, /device:TPU:1, one launch (start us, length us, event | category | flops | bytes accessed | tf_op | source)
XLA Modules:
  0.0 83.2 jit_solution(14127148362060238795)
XLA Ops:
  0.6 81.3 %shard_map.68 = (f32[16,128]{1,0:T(8,128)S(1)}, f32[128,128]{1,0:T(8,128)S(1)}) custom-call(bf16[2,128,128]{2,1,0:T(8,128)(2,1)} %bitcast.6, bf16[2,128,128]{2,1,0:T(8,128)(2,1)} %bitcast.7, bf16[4,1024,128]{2,1,0:T(8,128)(2,1)} %bitcast.5, f32[2,1,128]{2,1,0:T(1,128)} %bitcast.9, f32[4,8,128]{2,1,0:T(8,128)} %bitcast.8), custom_call_target="tpu_custom_call" | custom-call | tf_op jit(solution)/shard_map/pallas_call | solution.py:533
  82.0 0.6 copy.9
  82.6 0.6 copy.10

commit v6 on v5

--- a/solution.py
+++ b/solution.py
@@ -46,6 +46,14 @@
     return pl.ds(pl.multiple_of(i * size, size), size)
 
 
+def div(a, b):
+    return lax.div(a, jnp.int32(b))
+
+
+def rem(a, b):
+    return lax.rem(a, jnp.int32(b))
+
+
 def far_first(count):
     return sorted(range(1, count), key=lambda step: -min(step, count - step))
 
@@ -55,10 +63,10 @@
     nx, nyl, nc, nyh, nz = dims
     ny, nxc, npr = nyl * nyh, nx * nc, nx * nyl * nc
     row_id, me_p = lax.axis_index("row"), lax.axis_index("proto")
-    yh, z = row_id // nz, row_id % nz
-    core = me_p % nc
-    yl = (me_p // nc) % nyl
-    x = me_p // (nc * nyl)
+    yh, z = div(row_id, nz), rem(row_id, nz)
+    core = rem(me_p, nc)
+    yl = rem(div(me_p, nc), nyl)
+    x = div(me_p, nc * nyl)
     y = yh * nyl + yl
     xc = x * nc + core
 
@@ -69,10 +77,10 @@
         return (other * nz + z, me_p)
 
     def at_y(other):
-        return ((other // nyl) * nz + z, (x * nyl + other % nyl) * nc + core)
+        return (div(other, nyl) * nz + z, (x * nyl + rem(other, nyl)) * nc + core)
 
     def at_xc(other):
-        return (row_id, ((other // nc) * nyl + yl) * nc + other % nc)
+        return (row_id, (div(other, nc) * nyl + yl) * nc + rem(other, nc))
 
     def at_p(other):
         return (row_id, other)
@@ -104,10 +112,10 @@
         pro_load(part).start()
 
     barrier = pltpu.get_barrier_semaphore()
-    for count, me, address in ((nz, z, at_z), (ny, y, at_y), (npr, me_p, at_p)):
-        for step in range(1, count):
+    for count, me, address in ((ny, y, at_y), (nz, z, at_z), (npr, me_p, at_p)):
+        for step in far_first(count):
             pl.semaphore_signal(
-                barrier, inc=1, device_id=address((me + step) % count), device_id_type=MESH
+                barrier, inc=1, device_id=address(rem(me + step, count)), device_id_type=MESH
             )
     for load in small_loads:
         load.wait()
@@ -149,19 +157,19 @@
 
     def start(slots, me, count, address, send, recv):
         for step in far_first(count):
-            other = (me + step) % count
+            other = rem(me + step, count)
             pltpu.make_async_remote_copy(
                 slots.at[me], slots.at[me], send.at[step], recv.at[me], address(other), MESH
             ).start()
 
     def finish(slots, me, count, address, send, recv):
         for step in range(1, count):
-            other = (me + step) % count
+            other = rem(me + step, count)
             pltpu.make_async_remote_copy(
                 slots.at[other], slots.at[other], send.at[step], recv.at[other], address(other), MESH
             ).wait_recv()
         for step in range(1, count):
-            other = (me + step) % count
+            other = rem(me + step, count)
             pltpu.make_async_remote_copy(
                 slots.at[me], slots.at[me], send.at[step], recv.at[me], address(other), MESH
             ).wait_send()
@@ -169,7 +177,7 @@
     def scatter(shares, slots, me, count, address, send, recv):
         copies = []
         for step in far_first(count):
-            other = (me + step) % count
+            other = rem(me + step, count)
             copies.append(
                 pltpu.make_async_remote_copy(
                     shares.at[other], slots.at[me], send.at[step], recv.at[me], address(other), MESH
@@ -180,7 +188,7 @@
 
     def arrived(slots, me, count, address, send, recv):
         for step in range(1, count):
-            other = (me + step) % count
+            other = rem(me + step, count)
             pltpu.make_async_remote_copy(
                 slots.at[other], slots.at[other], send.at[step], recv.at[other], address(other), MESH
             ).wait_recv()
@@ -204,12 +212,13 @@
     start(m.bw, *along_p, m.w_send, m.w_recv)
 
     sign = 2 * yl - 1
-    partner = at_xc(x * nc + (core + 1) % nc)
+    partner = at_xc(x * nc + rem(core + 1, nc))
     blocks = []
     for step in range(1, nyh):
-        target = (y + sign * step + ny) % ny
-        source = (y + (sign if step % 2 else -sign) * step + ny) % ny
-        blocks.append((source // nyl, pl.ds((source // nyl) * per_block, per_block)))
+        target = rem(y + sign * step + ny, ny)
+        source = rem(y + (sign if step % 2 else -sign) * step + ny, ny)
+        origin = div(source, nyl)
+        blocks.append((origin, pl.ds(origin * per_block, per_block)))
         rows_out = pltpu.make_async_remote_copy(
             m.ev.at[core, own], m.ev.at[core, own], m.g_send.at[step], m.g_recv.at[step], at_y(target), MESH
         )
@@ -274,7 +283,7 @@
 
     def fill(step):
         block, there = blocks[step - 1]
-        taken = m.ev.at[(core + 1) % nc, there]
+        taken = m.ev.at[rem(core + 1, nc), there]
         scales = m.rs.at[there]
         pltpu.make_async_remote_copy(
             scales, scales, m.r_send.at[step], m.r_recv.at[step], partner, MESH
@@ -330,8 +339,8 @@
                 block = block + m.plan[rows, cols] * col_dual[g : g + 1, :]
             m.bx[k, xc, i : i + 1, :] = across(block)
 
-    def sweep(k, duals):
-        row_part(duals[1], k)
+    def sweep(k, col_dual):
+        row_part(col_dual, k)
         start(m.bx.at[k], *along_x, m.x_send, m.x_recv.at[k])
 
         @pl.when(k == 0)
@@ -356,78 +365,81 @@
         row_dual = (m.row_weight[...] - total(m.by.at[k], ny)) / m.row_mass[...]
         column_part(row_dual, k)
         start(m.bz.at[k], *along_z, m.z_send, m.z_recv.at[k + 1])
+
+        @pl.when(k == ITERS - 2)
+        def _():
+            m.dual[...] = row_dual * (1.0 / cot_scale)
+
+            @pl.loop(0, chunks)
+            def _(i):
+                rows = aligned(i)
+                dual = down(m.dual[pl.ds(i, 1), :])
+                for cols in tiles_of(groups):
+                    piece = m.plan[rows, cols] * (m.dot[rows, cols] - dual)
+                    m.dot[rows, cols] = piece * (cot_scale * logit_scale)
+
         finish(m.bz.at[k], *along_z, m.z_send, m.z_recv.at[k + 1])
-        return row_dual, (col_weight - total(m.bz.at[k], nz)) / col_mass
-
-    row_dual, col_dual = lax.fori_loop(
-        0, ITERS - 1, sweep, (jnp.zeros((chunks, LANES), F32), col_dual)
-    )
-
-    m.bx[0, xc] = row_dual * (1.0 / cot_scale)
-    col_scaled = col_dual * (1.0 / cot_scale)
-    half = nx // per_block
-
-    def last_chunk(block, h):
-        i = block * per_block + h
-        rows = aligned(i)
-        dual = down(m.bx[0, xc, pl.ds(i, 1), :])
-        for g, cols in enumerate(tiles_of(groups)):
-            piece = m.plan[rows, cols] * (m.dot[rows, cols] - dual - col_scaled[g : g + 1, :])
-            m.grad[rows, cols] = (cot_scale * logit_scale * piece).astype(BF16)
-        product = jnp.dot(m.grad[rows, :], m.pr[yh], preferred_element_type=F32)
-        m.eb[block, pl.ds(h * half, half)] = product.reshape(
-            half, nyl, nc, LANES // (half * nyl * nc), width
+        return (col_weight - total(m.bz.at[k], nz)) / col_mass
+
+    col_dual = lax.fori_loop(0, ITERS - 1, sweep, col_dual)
+
+    col_scaled = col_dual * logit_scale
+    span = nyh // 2
+    part_rows = span * per_block * LANES
+    for turn_half in range(2):
+        part = rem(div(yh, span) + 1 + turn_half, 2)
+
+        @pl.loop(0, span * per_block)
+        def _(i):
+            rows = aligned(part * (span * per_block) + i)
+            for g, cols in enumerate(tiles_of(groups)):
+                piece = m.dot[rows, cols] - m.plan[rows, cols] * col_scaled[g : g + 1, :]
+                m.grad[rows, cols] = piece.astype(BF16)
+
+        product = jnp.dot(m.grad[aligned(part, part_rows), :], m.pr[yh], preferred_element_type=F32)
+        m.eb[pl.ds(part * span, span)] = product.reshape(
+            span, nx, nyl, nc, m.eb.shape[4], width
         ).astype(BF16)
+        for low in range(span):
+            block = part * span + low
+            for turn in far_first(nxc):
+                other = rem(xc + turn, nxc)
+                sends.append(
+                    pltpu.make_async_remote_copy(
+                        m.eb.at[block, div(other, nc), :, rem(other, nc)],
+                        m.fx.at[block, xc],
+                        m.fx_send.at[turn_half * span + low, turn],
+                        m.fx_recv.at[block, xc],
+                        at_xc(other),
+                        MESH,
+                    )
+                )
+                sends[-1].start()
+
+    share = m.tail[...] + dot_tn(m.grad[...], m.ev[0].reshape(chunks * LANES, width))
+    m.tail[...] = share
+    m.pb[...] = share.reshape(m.pb.shape).astype(BF16)
+    for step in far_first(nz):
+        other = rem(z + step, nz)
+        sends.append(
+            pltpu.make_async_remote_copy(
+                m.pb.at[other], m.fz.at[z], m.fz_send.at[step], m.fz_recv.at[z], at_z(other), MESH
+            )
+        )
+        sends[-1].start()
 
     for step in range(1, nyh + 1):
-        block = (yh + step) % nyh
-
-        for h in range(per_block):
-            last_chunk(block, h)
-
-        for turn in range(1, nxc):
-            other = (xc + turn) % nxc
-            sends.append(
-                pltpu.make_async_remote_copy(
-                    m.eb.at[block, other // nc, :, other % nc],
-                    m.fx.at[block, xc],
-                    m.fx_send.at[step - 1, turn],
-                    m.fx_recv.at[block, xc],
-                    at_xc(other),
-                    MESH,
-                )
-            )
-            sends[-1].start()
-        if step < nyh:
-            m.tail[...] += dot_tn(m.grad[aligned(block, per_block * LANES), :], block_rows(0, block))
-
-    for step in far_first(nz) + [nz]:
-        other = (z + step) % nz
-        cols = aligned(other)
-        share = m.tail[cols, :] + dot_tn(m.grad[own_rows, cols], block_rows(0, yh))
-        if step < nz:
-            m.pb[step] = share.astype(BF16)
-            sends.append(
-                pltpu.make_async_remote_copy(
-                    m.pb.at[step], m.fz.at[z], m.fz_send.at[step], m.fz_recv.at[z], at_z(other), MESH
-                )
-            )
-            sends[-1].start()
-        else:
-            pg_ref[...] = share
-
-    for step in range(1, nyh + 1):
-        block = (yh + step) % nyh
+        block = rem(yh + step, nyh)
         arrived(m.fx.at[block], *along_x, m.fx_send.at[step - 1], m.fx_recv.at[block])
         part = m.eb[block, x, :, core].astype(F32)
         for turn in range(1, nxc):
-            part = part + m.fx[block, (xc + turn) % nxc].astype(F32)
+            part = part + m.fx[block, rem(xc + turn, nxc)].astype(F32)
         m.fy_out[pl.ds(block * nyl, nyl)] = part
         for low in range(nyl):
             if step < nyh:
                 other, slot = block * nyl + low, (step - 1) * nyl + low
             elif low:
-                other, slot = yh * nyl + (yl + low) % nyl, (step - 1) * nyl + low
+                other, slot = yh * nyl + rem(yl + low, nyl), (step - 1) * nyl + low
             else:
                 continue
             sends.append(
@@ -438,15 +450,15 @@
             sends[-1].start()
 
     arrived(m.fz, *along_z, m.fz_send, m.fz_recv)
-    share = pg_ref[...]
+    share = m.tail[aligned(z, m.fz.shape[1]), :]
     for step in range(1, nz):
-        share = share + m.fz[(z + step) % nz].astype(F32)
+        share = share + m.fz[rem(z + step, nz)].astype(F32)
     pg_ref[...] = share
 
     arrived(m.fy, *along_y, m.fy_send, m.fy_recv)
     rows_out = m.fy_out[y]
     for step in range(1, ny):
-        rows_out = rows_out + m.fy[(y + step) % ny]
+        rows_out = rows_out + m.fy[rem(y + step, ny)]
     eg_ref[...] = rows_out
 
     for send in sends:
@@ -484,6 +496,7 @@
             bw=vmem((npr, 2 * per_block, LANES), F32),
             rsum=vmem((nyh, 2 * per_block, LANES), F32),
             dual0=vmem((per_block, LANES), F32),
+            dual=vmem((chunks, LANES), F32),
             row_mass=vmem((chunks, LANES), F32),
             row_weight=vmem((chunks, LANES), F32),
             cms=vmem((nyh, 2, groups, LANES), F32),

time: 83.6 us -> 84.3 us (level)
  Pallas kernels: 81.3 us -> 82.2 us
    pallas_call x1, Pallas kernels: 81.3 us -> 82.2 us  [per_device(): pl.pallas_call(functools.partial(kernel, dims, proto_total, tuple(scratch...]
where the time goes in v6:
time: 84.3 us; the launch traced here: 84.1 us
  Pallas kernels  82.2 us (98%)
  local copies, waits for them, and re-layouts  1.23 us (1%)
    pallas_call x1, Pallas kernels, per_device(): pl.pallas_call(functools.partial(kernel, dims, proto_total, tuple(scratch...  82.2 us

profile of v6, /device:TPU:1, one launch (start us, length us, event | category | flops | bytes accessed | tf_op | source)
XLA Modules:
  0.0 84.1 jit_solution(15006150630104323564)
XLA Ops:
  0.6 82.2 %shard_map.68 = (f32[16,128]{1,0:T(8,128)S(1)}, f32[128,128]{1,0:T(8,128)S(1)}) custom-call(bf16[2,128,128]{2,1,0:T(8,128)(2,1)} %bitcast.6, bf16[2,128,128]{2,1,0:T(8,128)(2,1)} %bitcast.7, bf16[4,1024,128]{2,1,0:T(8,128)(2,1)} %bitcast.5, f32[2,1,128]{2,1,0:T(1,128)} %bitcast.9, f32[4,8,128]{2,1,0:T(8,128)} %bitcast.8), custom_call_target="tpu_custom_call" | custom-call | tf_op jit(solution)/shard_map/pallas_call | solution.py:546
  82.9 0.6 copy.9
  83.5 0.6 copy.10

commit v7 on v6

--- a/solution.py
+++ b/solution.py
@@ -151,8 +151,8 @@
             m.dot0[part] = dot_nt(block_rows(1, yh), m.pr[part])
             own_part(part)
 
-    own_parts(0, nyh // 2)
-    own_parts(nyh // 2, nyh)
+    for part in range(nyh):
+        own_parts(part, part + 1)
     sends = []
 
     def start(slots, me, count, address, send, recv):
@@ -384,38 +384,38 @@
     col_dual = lax.fori_loop(0, ITERS - 1, sweep, col_dual)
 
     col_scaled = col_dual * logit_scale
-    span = nyh // 2
-    part_rows = span * per_block * LANES
-    for turn_half in range(2):
-        part = rem(div(yh, span) + 1 + turn_half, 2)
-
-        @pl.loop(0, span * per_block)
-        def _(i):
-            rows = aligned(part * (span * per_block) + i)
+
+    def last_block(block):
+        for h in range(per_block):
+            rows = aligned(block * per_block + h)
             for g, cols in enumerate(tiles_of(groups)):
                 piece = m.dot[rows, cols] - m.plan[rows, cols] * col_scaled[g : g + 1, :]
                 m.grad[rows, cols] = piece.astype(BF16)
 
-        product = jnp.dot(m.grad[aligned(part, part_rows), :], m.pr[yh], preferred_element_type=F32)
-        m.eb[pl.ds(part * span, span)] = product.reshape(
-            span, nx, nyl, nc, m.eb.shape[4], width
-        ).astype(BF16)
-        for low in range(span):
-            block = part * span + low
-            for turn in far_first(nxc):
-                other = rem(xc + turn, nxc)
-                sends.append(
-                    pltpu.make_async_remote_copy(
-                        m.eb.at[block, div(other, nc), :, rem(other, nc)],
-                        m.fx.at[block, xc],
-                        m.fx_send.at[turn_half * span + low, turn],
-                        m.fx_recv.at[block, xc],
-                        at_xc(other),
-                        MESH,
-                    )
+    def send_block(step, block):
+        rows = aligned(block, per_block * LANES)
+        product = jnp.dot(m.grad[rows, :], m.pr[yh], preferred_element_type=F32)
+        m.eb[block] = product.reshape(m.eb.shape[1:]).astype(BF16)
+        for turn in range(1, nxc):
+            other = rem(xc + turn, nxc)
+            sends.append(
+                pltpu.make_async_remote_copy(
+                    m.eb.at[block, div(other, nc), :, rem(other, nc)],
+                    m.fx.at[block, xc],
+                    m.fx_send.at[step - 1, turn],
+                    m.fx_recv.at[block, xc],
+                    at_xc(other),
+                    MESH,
                 )
-                sends[-1].start()
-
+            )
+            sends[-1].start()
+
+    for step in range(1, nyh):
+        block = rem(yh + step, nyh)
+        last_block(block)
+        send_block(step, block)
+
+    last_block(yh)
     share = m.tail[...] + dot_tn(m.grad[...], m.ev[0].reshape(chunks * LANES, width))
     m.tail[...] = share
     m.pb[...] = share.reshape(m.pb.shape).astype(BF16)
@@ -427,6 +427,7 @@
             )
         )
         sends[-1].start()
+    send_block(nyh, yh)
 
     for step in range(1, nyh + 1):
         block = rem(yh + step, nyh)

time: 84.3 us -> 83 us (0.985)
  Pallas kernels: 82.2 us -> 81 us
    pallas_call x1, Pallas kernels: 82.2 us -> 81 us  [per_device(): pl.pallas_call(functools.partial(kernel, dims, proto_total, tuple(scratch...]
where the time goes in v7:
time: 83 us; the launch traced here: 82.8 us
  Pallas kernels  81 us (98%)
  local copies, waits for them, and re-layouts  1.23 us (1%)
    pallas_call x1, Pallas kernels, per_device(): pl.pallas_call(functools.partial(kernel, dims, proto_total, tuple(scratch...  81 us

profile of v7, /device:TPU:1, one launch (start us, length us, event | category | flops | bytes accessed | tf_op | source)
XLA Modules:
  0.0 82.8 jit_solution(12928977852992379587)
XLA Ops:
  0.6 81.0 %shard_map.68 = (f32[16,128]{1,0:T(8,128)S(1)}, f32[128,128]{1,0:T(8,128)S(1)}) custom-call(bf16[2,128,128]{2,1,0:T(8,128)(2,1)} %bitcast.6, bf16[2,128,128]{2,1,0:T(8,128)(2,1)} %bitcast.7, bf16[4,1024,128]{2,1,0:T(8,128)(2,1)} %bitcast.5, f32[2,1,128]{2,1,0:T(1,128)} %bitcast.9, f32[4,8,128]{2,1,0:T(8,128)} %bitcast.8), custom_call_target="tpu_custom_call" | custom-call | tf_op jit(solution)/shard_map/pallas_call | solution.py:547
  81.6 0.6 copy.9
  82.2 0.6 copy.10
